TPU v7x, 512 devices: a whole 4x8x8 slice. The times are simulated.
512 devices in a mesh: seq: 64 (over x, z, y_hi), head: 8 (over y_lo, core).
Axes of the slice: x: 4, y: 8 (y_hi: 2, y_lo: 4; y = y_hi * 4 + y_lo), z: 8, core: 2. Of those that a mesh axis runs over, the one named last changes fastest.
Arguments:
- layer_input: bfloat16 [8192, 4096], P('seq', 'head'), may hold values from -16 to 16
- query_rows: bfloat16 [8192, 2048], P('seq', 'head'), may hold values from -6 to 6
- key_matrix_rows: bfloat16 [8192, 2048], P('seq', 'head'), may hold values from -1.25 to 1.25
- value_rows: bfloat16 [8192, 2048], P('seq', 'head'), may hold values from -6 to 6
- beta_rows: float32 [8192, 16], P('seq', 'head'), may hold values from 0 to 0.9, as said below
- log_gate: float32 [8192, 16], P('seq', 'head'), may hold values from -1.3 to 0, as said below
- grad_out: bfloat16 [8192, 2048], P('seq', 'head'), may hold values from -6 to 6
Outputs:
- grad_query: bfloat16 [8192, 2048], P('seq', 'head')
- grad_key: bfloat16 [8192, 2048], P('seq', 'head')
- grad_value: bfloat16 [8192, 2048], P('seq', 'head')
- grad_beta: float32 [8192, 16], P('seq', 'head')
- grad_log_gate: float32 [8192, 16], P('seq', 'head')
- grad_weight: bfloat16 [4096, 2048], P(None, 'head')
Inputs may be any that keep to these rules, and one draw needn't show every extreme that they name: `beta_rows`: write strengths vary from token to token and from head to head. `log_gate`: decay rates vary from token to token and from head to head.
All inputs are finite; a program needn't handle non-finite values.
Results may differ from a plain program's by a relative error of at most 0.0049.
Values may be sent and summed in bfloat16 or wider, within the bound.
A program may use at most 128 MiB of HBM per device.

v0:
```python
from functools import partial

import jax
import jax.numpy as jnp
from jax import lax
from jax.sharding import PartitionSpec as P

HD = 128
BLOCK = 64


HIGHEST_PRECISION = lax.Precision.HIGHEST


def carried_in(part, axis, combine, identity, reverse):
    count = lax.axis_size(axis)
    place = lax.axis_index(axis)
    ahead = count - 1 - place if reverse else place
    gathered = jax.tree.map(lambda a: lax.all_gather(a, axis), part)
    state = jax.tree.map(lambda a, e: jnp.zeros_like(a) + jnp.asarray(e, a.dtype), part, identity)

    def one(turn, state):
        source = count - 1 - turn if reverse else turn
        return combine(
            state, jax.tree.map(lambda a: lax.dynamic_index_in_dim(a, source, 0, False), gathered)
        )

    return lax.fori_loop(0, ahead, one, state)


def product(left_side, right_side):
    return jnp.matmul(left_side, right_side, precision=HIGHEST_PRECISION)


def flipped(matrix):
    return jnp.swapaxes(matrix, -1, -2)


def unit_inverse(strict_lower):
    order_size = strict_lower.shape[-1]
    identity = jnp.eye(order_size, dtype=strict_lower.dtype)
    result = identity - strict_lower
    exponent_summand = strict_lower
    covered = 2
    while covered < order_size:
        exponent_summand = product(exponent_summand, exponent_summand)
        result = product(result, identity + exponent_summand)
        covered = covered * 2
    return result


def block_parts(key_block, strength, log_decay):
    order_size = log_decay.shape[-1]
    running = jnp.cumsum(log_decay, axis=-1)
    line_number = lax.broadcasted_iota(jnp.int32, (order_size, order_size), 0)
    col_index = lax.broadcasted_iota(jnp.int32, (order_size, order_size), 1)
    causal = line_number >= col_index
    strict = line_number > col_index
    spread = running[..., :, None] - running[..., None, :]
    decay_table = jnp.where(causal, jnp.exp(jnp.where(causal, spread, 0.0)), 0.0)
    strict_lower = jnp.where(
        strict, strength[..., :, None] * decay_table * product(key_block, flipped(key_block)), 0.0
    )
    growth = jnp.exp(running)
    tail_decay = jnp.exp(running[..., -1:] - running)
    return (decay_table, growth, tail_decay, unit_inverse(strict_lower))


def segment(query_block, key_block, value_block, strength, log_decay, init_state, with_out):
    decay_table, growth, tail_decay, inverse = block_parts(key_block, strength, log_decay)
    pseudo = product(inverse, strength[..., None] * value_block)
    erasure = product(inverse, (strength * growth)[..., None] * key_block)
    written = flipped(tail_decay[..., None] * key_block)
    keep_all = growth[..., -1]
    argument_sequence = [pseudo, erasure, written, keep_all]
    if with_out:
        argument_sequence = argument_sequence + [
            decay_table * product(query_block, flipped(key_block)),
            growth[..., None] * query_block,
        ]

    def advance(carry_state, pieces):
        update = pieces[0] - product(pieces[1], carry_state)
        after_state = pieces[3] * carry_state + product(pieces[2], update)
        if with_out:
            return (after_state, product(pieces[5], carry_state) + product(pieces[4], update))
        return (after_state, None)

    return lax.scan(advance, init_state, tuple(argument_sequence))


def combine_maps(earlier, later):
    return (product(later[0], earlier[0]), product(later[0], earlier[1]) + later[1])


def shards(layer_input, query_rows, key_matrix_rows, value_rows, beta_rows, log_gate, grad_out):
    length = query_rows.shape[0]
    heads_here = beta_rows.shape[1]
    block_count = length // BLOCK

    def per_head_apply(matrix):
        return (
            matrix.reshape(block_count, BLOCK, heads_here, HD)
            .transpose(2, 0, 1, 3)
            .astype(jnp.float32)
        )

    def by_head_scalar(matrix):
        return matrix.reshape(block_count, BLOCK, heads_here).transpose(2, 0, 1)

    def to_rows(tensor):
        return tensor.transpose(1, 2, 0, 3).reshape(length, heads_here * HD).astype(jnp.bfloat16)

    queries = per_head_apply(query_rows)
    keys_local = per_head_apply(key_matrix_rows)
    values_local = per_head_apply(value_rows)
    grads_local = per_head_apply(grad_out)
    strength = by_head_scalar(beta_rows)
    decays = by_head_scalar(log_gate)
    run_states = jax.vmap(partial(segment, with_out=False))
    run_full = jax.vmap(partial(segment, with_out=True))
    identity = jnp.broadcast_to(jnp.eye(HD, dtype=jnp.float32), (heads_here, HD, HD))
    zero_state = jnp.zeros((heads_here, HD, HD), jnp.float32)
    stacked_start = jnp.concatenate([identity, zero_state], axis=2)
    widened = jnp.concatenate([jnp.zeros_like(values_local), values_local], axis=3)
    combined, unused = run_states(queries, keys_local, widened, strength, decays, stacked_start)
    transit = combined[:, :, :HD]
    offset = combined[:, :, HD:]

    def local_outputs(state_guess):
        return run_full(queries, keys_local, values_local, strength, decays, state_guess)[1]

    unused_out, pull_state = jax.vjp(local_outputs, zero_state)
    carried = pull_state(grads_local)[0]
    unused_map, entry_state = carried_in(
        (transit, offset), "seq", combine_maps, (identity, zero_state), False
    )
    unused_back, leaving = carried_in(
        (flipped(transit), carried), "seq", combine_maps, (identity, zero_state), True
    )

    def whole_layer(query_all, key_all, value_all, strength_all, decay_all):
        return run_full(query_all, key_all, value_all, strength_all, decay_all, entry_state)

    unused_pair, pull_back = jax.vjp(
        whole_layer, queries, keys_local, values_local, strength, decays
    )
    gradients = pull_back((leaving, grads_local))
    grad_value = to_rows(gradients[2])
    grad_beta = gradients[3].transpose(1, 2, 0).reshape(length, heads_here)
    grad_log_gate = gradients[4].transpose(1, 2, 0).reshape(length, heads_here)
    summand = jnp.einsum(
        "tc,th->ch",
        lax.all_gather(layer_input, "head", axis=1, tiled=True),
        grad_value,
        preferred_element_type=jnp.float32,
    )
    grad_weight = lax.psum(summand, "seq").astype(jnp.bfloat16)
    return (
        to_rows(gradients[0]),
        to_rows(gradients[1]),
        grad_value,
        grad_beta,
        grad_log_gate,
        grad_weight,
    )


def solution(mesh):
    in_specs = (
        P("seq", "head"),
        P("seq", "head"),
        P("seq", "head"),
        P("seq", "head"),
        P("seq", "head"),
        P("seq", "head"),
        P("seq", "head"),
    )
    out_specs = (
        P("seq", "head"),
        P("seq", "head"),
        P("seq", "head"),
        P("seq", "head"),
        P("seq", "head"),
        P(None, "head"),
    )
    return jax.shard_map(shards, mesh=mesh, in_specs=in_specs, out_specs=out_specs, check_vma=False)
```

profile of v0, /device:TPU:52, one launch (start us, length us, event | category | flops | bytes accessed | tf_op | source)
XLA Modules:
  0.0 1518.6 jit_solution(11103032248653186808)
XLA Ops:
  17.7 1.5 while.103
  22.6 2.6 while.109
  28.1 183.8 %all-gather.16.cloned.1.call-done = f32[128,128,128]{2,1,0:T(8,128)} async-done(((f32[2,128,128]{2,1,0:T(8,128)}), f32[128,128,128]{2,1,0:T(8,128)}) %all-gather.16.cloned.1.call-update) | async-done | bytes 8388624 | tf_op jit(solution)/shard_map/all_gather | solution.py:19
  211.9 188.0 %all-gather.18.cloned.1.call-done = f32[128,128,128]{2,1,0:T(8,128)} async-done(((f32[2,128,128]{2,1,0:T(8,128)}), f32[128,128,128]{2,1,0:T(8,128)}) %all-gather.18.cloned.1.call-update) | async-done | bytes 8388624 | tf_op jit(solution)/shard_map/all_gather | solution.py:19
  400.0 42.6 %while.106 = (s32[]{:T(128)}, f32[2,128,128]{2,1,0:T(8,128)S(1)}, s32[]{:T(128)}, f32[64,2,128,128]{3,2,1,0:T(8,128)}, f32[64,2,128,128]{3,2,1,0:T(8,128)}, /*index=5*/s32[]{:T(128)}, s32[]{:T(128)}, s32[]{:T(128)}) while((s32[]{:T(128)}, f32[2,128,128]{2,1,0:T(8,128)S(1)}, s32[]{:T(128)}, f32[64,2,128,128]{3,2,1,0:T(8,128)}, ...), condition=%wide.region_10.11_spmd, body=%wide.region_9.10_spmd.sunk | while | flops 50364420 | bytes 787575 | solution.py:28
  415.5 1.2 convolution_add_fusion.31
  416.8 1.2 convolution_add_fusion.31
  423.3 1.2 convolution_add_fusion.31
  424.6 1.2 convolution_add_fusion.31
  429.7 1.2 convolution_add_fusion.31
  438.8 1.2 convolution_add_fusion.31
  442.6 1.5 while.107
  444.1 144.1 %all-gather.14.cloned.1.call-done = f32[128,128,128]{2,1,0:T(8,128)} async-done(((f32[2,128,128]{2,1,0:T(8,128)}), f32[128,128,128]{2,1,0:T(8,128)}) %all-gather.14.cloned.1.call-update) | async-done | bytes 8388624 | tf_op jit(solution)/shard_map/all_gather | solution.py:19
  588.3 188.5 %all-gather.12.cloned.1.call-done = f32[128,128,128]{2,1,0:T(8,128)} async-done(((f32[2,128,128]{2,1,0:T(8,128)}), f32[128,128,128]{2,1,0:T(8,128)}) %all-gather.12.cloned.1.call-update) | async-done | bytes 8388624 | tf_op jit(solution)/shard_map/all_gather | solution.py:19
  776.7 38.8 %while.105 = (s32[]{:T(128)}, f32[2,128,128]{2,1,0:T(8,128)S(1)}, s32[]{:T(128)}, f32[64,2,128,128]{3,2,1,0:T(8,128)}, f32[64,2,128,128]{3,2,1,0:T(8,128)}, /*index=5*/s32[]{:T(128)}, s32[]{:T(128)}, s32[]{:T(128)}, s32[]{:T(128)}) while((s32[]{:T(128)}, f32[2,128,128]{2,1,0:T(8,128)S(1)}, s32[]{:T(128)}, f32[64,2,128,128]{3,2,1,0:T(8,128)}, ...), condition=%wide.region_8.9_spmd, body=%wide.region_7.8_spmd.sunk | while | flops 50364420 | bytes 787595 | solution.py:28
  797.5 1.2 convolution_add_fusion.30
  816.3 6.8 while.108
  826.0 3.9 convolution_bitcast_fusion.4
  829.9 660.0 %all-reduce.5 = bf16[4096,256]{0,1:T(8,128)(2,1)S(1)} all-reduce(f32[4096,256]{0,1:T(8,128)} %convolution_bitcast_fusion.4), channel_id=1, replica_groups=mesh['seq'=64,'head'=8] {'seq'}, use_global_device_ids=true, to_apply=%region_25.26 | all-reduce | flops 1048576 | bytes 6291456 | tf_op jit(solution)/shard_map/psum | solution.py:158
  1489.9 2.5 copy.242
  1492.4 1.5 fusion.98
  1498.5 1.4 convolution_add_fusion.17
  1500.6 1.3 convolution_add_fusion.15
  1502.6 1.3 convolution_add_fusion.13
  (319 shorter events, 116.1 us)
Async XLA Ops:
  7.2 204.7 %all-gather.16.cloned.1.call-start = ((), (), s32[]{:S(2)}) async-start(), calls=%async_computation.3 | async-start | bytes 8519680 | tf_op jit(solution)/shard_map/all_gather | solution.py:19
  8.8 12.8 copy-start.14
  11.2 11.1 copy-start.13
  11.3 15.7 %copy-start.1 = (f32[2,2,64,64]{2,3,1,0:T(8,128)}, f32[2,2,64,64]{2,3,1,0:T(8,128)S(1)}, u32[]{:S(2)}) copy-start(f32[2,2,64,64]{2,3,1,0:T(8,128)S(1)} %copy.169) | copy-start | bytes 196612
  11.7 3.8 copy-start.2
  12.2 804.1 %copy-start.3 = (f32[2,2,64,64]{2,3,1,0:T(8,128)}, f32[2,2,64,64]{2,3,1,0:T(8,128)S(1)}, u32[]{:S(2)}) copy-start(f32[2,2,64,64]{2,3,1,0:T(8,128)S(1)} %copy.173) | copy-start | bytes 196612
  13.1 1.0 copy-start.9
  14.5 0.7 copy-start.6
  15.5 7.1 copy-start.7
  20.8 379.2 %all-gather.18.cloned.1.call-start = ((), (), s32[]{:S(2)}) async-start(), calls=%async_computation.4 | async-start | bytes 8519680 | tf_op jit(solution)/shard_map/all_gather | solution.py:19
  21.5 566.7 %all-gather.14.cloned.1.call-start = ((), (), s32[]{:S(2)}) async-start(), calls=%async_computation.2 | async-start | bytes 8519680 | tf_op jit(solution)/shard_map/all_gather | solution.py:19
  25.2 0.6 copy-start
  25.8 750.9 %all-gather.12.cloned.1.call-start = ((), (), s32[]{:S(2)}) async-start(), calls=%async_computation.1 | async-start | bytes 8519680 | tf_op jit(solution)/shard_map/all_gather | solution.py:19
  26.4 799.6 %all-gather.10.cloned.1.call-start = ((), (), s32[]{:S(2)}) async-start(), calls=%async_computation | async-start | bytes 1179648 | tf_op jit(solution)/shard_map/all_gather | solution.py:154
  823.1 0.7 copy-start.4
  823.1 2.9 copy-start.8
  823.8 668.5 %copy-start.12 = (bf16[16,8,2,128]{3,1,2,0:T(8,128)(2,1)}, bf16[16,8,2,128]{3,1,2,0:T(8,128)(2,1)S(1)}, u32[]{:S(2)}) copy-start(bf16[16,8,2,128]{3,1,2,0:T(8,128)(2,1)S(1)} %copy.359) | copy-start | bytes 196612
  1492.3 13.6 copy-start.10
  1492.3 14.2 copy-start.11
  1492.3 16.3 %copy-start.5 = (f32[2,2,128,64]{2,3,0,1:T(8,128)S(1)}, f32[2,2,128,64]{2,3,0,1:T(8,128)}, u32[]{:S(2)}) copy-start(f32[2,2,128,64]{2,3,0,1:T(8,128)} %copy-done.4) | copy-start | bytes 393220
Sparse Core Ops, SparseCore 0:
  20.9 190.9 all-gather.15
  216.4 183.5 all-gather.17
  404.4 183.7 all-gather.13
  593.2 183.5 all-gather.11
  778.7 29.6 all-gather.9
where the time goes:
time: 1520 us
  waiting for transfers between devices  706 us (46%)
  blocking collectives  660 us (43%)
  matrix products  116 us (8%)
  local copies, waits for them, and re-layouts  16.1 us (1%)
    all_gather x4, waiting for transfers between devices, carried_in(): gathered = jax.tree.map(lambda a: lax.all_gather(a, axis), part)  704 us
    psum x1, blocking collectives, shards(): grad_weight = lax.psum(summand, 'seq').astype(jnp.bfloat16)  660 us
    dot_general x138, matrix products, product(): return jnp.matmul(left_side, right_side, precision=HIGHEST_PRECISION)  112 us
  transfers between devices with their start and end apart: 5, of which 4 were waited for; matrix products, arithmetic and copies ran while one was open for 6% of the time, Pallas kernels for 0%

commit v1 on v0

v1 whole, which is shorter than its diff:
```python
import jax
import jax.numpy as jnp
from jax import lax
from jax.experimental import pallas as pl
from jax.experimental.pallas import tpu as pltpu
from jax.sharding import PartitionSpec as P

HD = 128
T = 128
F32 = jnp.float32
BF16 = jnp.bfloat16
HIGHEST = lax.Precision.HIGHEST
NY = 2


def dot(a, b, ca=1, cb=0):
    return lax.dot_general(
        a, b, (((ca,), (cb,)), ((), ())), precision=HIGHEST, preferred_element_type=F32
    )


def dot_exact(a, b, ca=1, cb=0):
    return lax.dot_general(a, b, (((ca,), (cb,)), ((), ())), preferred_element_type=F32)


def iotas():
    return (
        lax.broadcasted_iota(jnp.int32, (T, T), 0),
        lax.broadcasted_iota(jnp.int32, (T, T), 1),
    )


def unit_inverse(strict_lower):
    line, col = iotas()
    same = (line >= 64) == (col >= 64)
    diag_part = jnp.where(same, strict_lower, 0.0)
    below = jnp.where(same, 0.0, strict_lower)
    inverse = jnp.where(line == col, 1.0, 0.0) - diag_part
    power = dot(diag_part, diag_part)
    covered = 4
    while covered < 64:
        both = dot(jnp.concatenate([power, inverse], 0), power)
        inverse = inverse + both[T:]
        power = both[:T]
        covered = covered * 2
    inverse = inverse + dot(inverse, power)
    return inverse - dot(dot(inverse, below), inverse)


def gate_parts(lg):
    line, col = iotas()
    lg_row = jnp.sum(jnp.where(line == col, lg, 0.0), axis=0, keepdims=True)
    run_col = jnp.sum(jnp.where(col <= line, lg_row, 0.0), axis=1, keepdims=True)
    run_row = jnp.sum(jnp.where(line <= col, lg, 0.0), axis=0, keepdims=True)
    total = jnp.sum(lg, axis=0, keepdims=True)
    causal = line >= col
    decay = jnp.where(causal, jnp.exp(jnp.where(causal, run_col - run_row, 0.0)), 0.0)
    return decay, jnp.exp(run_col), jnp.exp(total - run_col), jnp.exp(total)


def local_maps(q, k, v, do, beta, lg):
    line, col = iotas()
    decay, growth, tail, keep = gate_parts(lg)
    keys = k.astype(F32)
    scores = decay * dot_exact(q, k, 1, 1)
    lower = beta * jnp.where(line > col, decay * dot_exact(k, k, 1, 1), 0.0)
    inverse = unit_inverse(lower)
    uw = dot(inverse, jnp.concatenate([beta * v.astype(F32), (beta * growth) * keys], 1))
    back = dot(scores, do.astype(F32), 0, 0)
    bw = dot(tail * keys, uw, 0, 0)
    eye = jnp.where(line == col, 1.0, 0.0)
    a = keep * eye - bw[:, HD:]
    b = bw[:, :HD]
    c = dot(growth * q.astype(F32), do.astype(F32), 0, 0) - dot(uw[:, HD:], back, 0, 0)
    return (a, b, c), (inverse, uw, back)


def local_grads(q, k, v, do, beta, lg, inverse, uw, back, state, adj):
    line, col = iotas()
    decay, growth, tail, keep = gate_parts(lg)
    queries, keys, values, grads = (m.astype(F32) for m in (q, k, v, do))
    update = uw[:, :HD] - dot(uw[:, HD:], state)
    d_update = back + dot(tail * keys, adj)
    e = dot(inverse, d_update, 0, 0)
    de = jnp.concatenate([grads, e], 0)
    by_state = dot(de, state, 1, 1)
    by_update = dot(de, update, 1, 1)
    nz = dot(update, adj, 1, 1)
    y = decay * by_update[:T]
    xp = -jnp.where(line > col, decay * by_update[T:], 0.0)
    by_key = dot(jnp.concatenate([xp, y], 0), keys)
    r = by_key[:T] - growth * by_state[T:]
    crossed = dot(
        jnp.concatenate([beta * xp, y], 0), jnp.concatenate([keys, queries], 0), 0, 0
    )
    dq = growth * by_state[:T] + by_key[T:]
    tail_nz = tail * nz
    dk_col = crossed + tail_nz
    dk_row = beta * r
    dv = beta * e
    d_beta = jnp.sum(e * values + keys * r, axis=1, keepdims=True)
    d_run = jnp.sum(queries * dq + keys * (dk_row - dk_col), axis=1, keepdims=True)
    last = jnp.sum(tail_nz * keys, axis=(0, 1), keepdims=True) + keep * jnp.sum(
        adj * state, axis=(0, 1), keepdims=True
    )
    d_run_row = jnp.sum(jnp.where(line == col, d_run, 0.0), axis=0, keepdims=True)
    d_lg = jnp.sum(jnp.where(col >= line, d_run_row, 0.0), axis=1, keepdims=True) + last
    return dq, dk_row + dk_col, dv, d_beta, d_lg


def head_of(ref, h):
    return ref[:, h * HD : (h + 1) * HD]


def maps_kernel(q, k, v, do, beta, lg, maps, inverse, uw, back):
    for h in range(2):
        (a, b, c), (inv, u, f) = local_maps(
            head_of(q, h), head_of(k, h), head_of(v, h), head_of(do, h),
            beta[:, h : h + 1], lg[:, h : h + 1],
        )
        maps[h, 0:HD] = a
        maps[h, HD : 2 * HD] = b
        maps[h, 2 * HD : 3 * HD] = c
        inverse[h] = inv
        uw[h] = u
        back[h] = f


def grads_kernel(q, k, v, do, beta, lg, inverse, uw, back, sz, dq, dk, dv, d_beta, d_lg):
    betas, lgs = [], []
    for h in range(2):
        gq, gk, gv, gb, gl = local_grads(
            head_of(q, h), head_of(k, h), head_of(v, h), head_of(do, h),
            beta[:, h : h + 1], lg[:, h : h + 1],
            inverse[h], uw[h], back[h], sz[h, 0:HD], sz[h, HD : 2 * HD],
        )
        dq[:, h * HD : (h + 1) * HD] = gq.astype(BF16)
        dk[:, h * HD : (h + 1) * HD] = gk.astype(BF16)
        dv[:, h * HD : (h + 1) * HD] = gv.astype(BF16)
        betas.append(gb)
        lgs.append(gl)
    d_beta[...] = jnp.concatenate(betas, 1)
    d_lg[...] = jnp.concatenate(lgs, 1)


class Place:
    def __init__(self, nx, nz):
        s = lax.axis_index("seq")
        self.nx, self.nz = nx, nz
        self.x = s // (nz * NY)
        self.z = lax.rem(s // NY, nz)
        self.y = lax.rem(s, NY)

    def at(self, x=None, z=None, y=None):
        x = self.x if x is None else x
        z = self.z if z is None else z
        y = self.y if y is None else y
        return {"seq": (x * self.nz + z) * NY + y}

    def right(self):
        return self.at(z=lax.rem(self.z + 1, self.nz))

    def left(self):
        return self.at(z=lax.rem(self.z + self.nz - 1, self.nz))

    def partner(self):
        return self.at(y=1 - self.y)

    def other_x(self, t):
        return lax.rem(self.x + t, self.nx)

    def greet(self):
        barrier = pltpu.get_barrier_semaphore()
        peers = [self.partner(), self.right(), self.left()]
        peers += [self.at(x=self.other_x(t)) for t in range(1, self.nx)]
        for peer in peers:
            pl.semaphore_signal(
                barrier, inc=1, device_id=peer, device_id_type=pl.DeviceIdType.MESH
            )
        pl.semaphore_wait(barrier, len(peers))


def remote(src, dst, send, recv, device):
    return pltpu.make_async_remote_copy(
        src_ref=src, dst_ref=dst, send_sem=send, recv_sem=recv,
        device_id=device, device_id_type=pl.DeviceIdType.MESH,
    )


def ring_z(place, view, rows, ssem, rsem):
    nz, z = place.nz, place.z
    steps = nz // 2
    sent = []
    before = [None, None]
    for t in range(1, steps + 1):
        start, count = (0, rows) if t < steps else (0, rows // 2)
        src = view(lax.rem(z + nz - t + 1, nz), start, count)
        if before[0] is not None:
            before[0].wait_recv()
        before[0] = remote(src, src, ssem.at[0, t - 1], rsem.at[0, t - 1], place.right())
        before[0].start()
        start, count = (0, rows) if t < steps else (rows // 2, rows // 2)
        src = view(lax.rem(z + t - 1, nz), start, count)
        if before[1] is not None:
            before[1].wait_recv()
        before[1] = remote(src, src, ssem.at[1, t - 1], rsem.at[1, t - 1], place.left())
        before[1].start()
        sent += before
    before[0].wait_recv()
    before[1].wait_recv()
    for copy in sent:
        copy.wait_send()


def chains(blocks, count, forth, aback):
    width = forth.shape[2] - HD

    def step(n, carry):
        m = count - 1 - n
        new = dot(blocks[n, 0:HD], forth[n])
        old = dot(blocks[m, 0:HD], aback[m + 1], 0, 0)
        if width:
            forth[n + 1, :, 0:width] = new[:, :width]
            aback[m, :, 0:width] = old[:, :width]
        forth[n + 1, :, width:] = new[:, width:] + blocks[n, HD : 2 * HD]
        aback[m, :, width:] = old[:, width:] + blocks[m, 2 * HD : 3 * HD]
        return carry

    lax.fori_loop(0, count, step, 0)


def scan_kernel(
    nx, nz, maps, sz, pair, zbuf, xbuf, zf, zb, xf, xb, both, s1, r1, zs, zr, xs, xr, s2, r2
):
    place = Place(nx, nz)
    x, z, y = place.x, place.z, place.y
    place.greet()
    first = remote(maps.at[1 - y], pair.at[y], s1, r1, place.partner())
    first.start()
    pair[y] = maps[y]
    line, col = iotas()
    eye = jnp.where(line == col, 1.0, 0.0)
    zero = jnp.zeros((HD, HD), F32)
    for ref, slot in ((zf, 0), (zb, nz)):
        ref[slot, :, 0:HD] = eye
        ref[slot, :, HD:] = zero
    xf[0] = zero
    xb[nx] = zero
    first.wait_recv()
    a0, a1 = pair[0, 0:HD], pair[1, 0:HD]
    ab = dot(a1, jnp.concatenate([a0, pair[0, HD : 2 * HD]], 1))
    zbuf[z, 0:HD] = ab[:, :HD]
    zbuf[z, HD : 2 * HD] = ab[:, HD:] + pair[1, HD : 2 * HD]
    zbuf[z, 2 * HD : 3 * HD] = pair[0, 2 * HD : 3 * HD] + dot(a0, pair[1, 2 * HD : 3 * HD], 0, 0)
    ring_z(place, lambda slot, start, count: zbuf.at[slot, pl.ds(start, count)], 3 * HD, zs, zr)
    chains(zbuf, nz, zf, zb)
    xbuf[x, 0:HD] = zf[nz, :, 0:HD]
    xbuf[x, HD : 2 * HD] = zf[nz, :, HD:]
    xbuf[x, 2 * HD : 3 * HD] = zb[0, :, HD:]
    copies = []
    for t in range(1, nx):
        copy = remote(
            xbuf.at[x], xbuf.at[x], xs.at[t - 1], xr.at[t - 1], place.at(x=place.other_x(t))
        )
        copy.start()
        copies.append(copy)
    for copy in copies:
        copy.wait_recv()
    chains(xbuf, nx, xf, xb)
    state = dot(zf[z, :, 0:HD], xf[x]) + zf[z, :, HD:]
    adj = dot(zb[z + 1, :, 0:HD], xb[x + 1]) + zb[z + 1, :, HD:]
    both[0, 0:HD] = state
    both[0, HD : 2 * HD] = dot(pair[1, 0:HD], adj, 0, 0) + pair[1, 2 * HD : 3 * HD]
    both[1, 0:HD] = dot(pair[0, 0:HD], state) + pair[0, HD : 2 * HD]
    both[1, HD : 2 * HD] = adj
    last = remote(both.at[1 - y], sz.at[y], s2, r2, place.partner())
    last.start()
    sz[y] = both[y]
    first.wait_send()
    for copy in copies:
        copy.wait_send()
    last.wait()


def weight_kernel(nx, nz, gv, xg, out, gbuf, psend, precv, ybuf, gs, gr, ps, pr, ys, yr, as_, ar, zs, zr):
    place = Place(nx, nz)
    x, z, y = place.x, place.z, place.y
    place.greet()
    gbuf[z] = gv[...]
    ring_z(place, lambda slot, start, count: gbuf.at[slot, pl.ds(start, count)], T, gs, gr)
    feats = xg.shape[1]
    piece = feats // nx
    cols = gv.shape[1]
    for n in range(nx):
        total = dot_exact(
            xg[:, n * piece : (n + 1) * piece], gbuf[...].reshape(nz * T, cols), 0, 0
        )
        psend[n] = total.astype(BF16)
    copies = []
    for t in range(1, nx):
        other = place.other_x(t)
        copy = remote(psend.at[other], precv.at[x], ps.at[t - 1], pr.at[t - 1], place.at(x=other))
        copy.start()
        copies.append(copy)
    precv[x] = psend[x]
    for copy in copies:
        copy.wait_recv()
    total = precv[0].astype(F32)
    for n in range(1, nx):
        total = total + precv[n].astype(F32)
    ybuf[y] = total.astype(BF16)
    over = remote(ybuf.at[y], ybuf.at[y], ys, yr, place.partner())
    over.start()
    over.wait_recv()
    mine = pl.ds(pl.multiple_of(z * feats + x * piece, piece), piece)
    out[mine] = (ybuf[0].astype(F32) + ybuf[1].astype(F32)).astype(BF16)
    for t in range(1, nx):
        copy = remote(
            out.at[mine], out.at[mine], as_.at[t - 1], ar.at[t - 1], place.at(x=place.other_x(t))
        )
        copy.start()
        copies.append(copy)
    for copy in copies[nx - 1 :]:
        copy.wait_recv()
    ring_z(
        place,
        lambda slot, start, count: out.at[pl.ds(pl.multiple_of(slot * feats + start, 128), count)],
        feats, zs, zr,
    )
    over.wait_send()
    for copy in copies:
        copy.wait_send()


def vmem(count):
    return [pl.BlockSpec(memory_space=pltpu.VMEM)] * count


def shards(nx, nz, layer_input, q, k, v, beta, lg, do):
    heads = nz
    ranks = []
    for s in range(nx * nz * NY):
        x, z, y = s // (nz * NY), (s // NY) % nz, s % NY
        for h in range(heads):
            ranks.append((s * heads + h, ((x * nz + h) * NY + y) * heads + z))
    moved = lax.ppermute(layer_input, ("seq", "head"), ranks)
    xg = lax.all_gather(moved, "head", axis=0, tiled=True)
    sd = jax.ShapeDtypeStruct
    maps, inverse, uw, back = pl.pallas_call(
        maps_kernel,
        out_shape=(
            sd((2, 3 * HD, HD), F32), sd((2, T, T), F32), sd((2, T, 2 * HD), F32), sd((2, T, HD), F32),
        ),
        in_specs=vmem(6), out_specs=tuple(vmem(4)), name="maps",
    )(q, k, v, do, beta, lg)
    dma = pltpu.SemaphoreType.DMA
    sz = pl.pallas_call(
        lambda *refs: scan_kernel(nx, nz, *refs),
        out_shape=sd((2, 2 * HD, HD), F32),
        in_specs=vmem(1), out_specs=vmem(1)[0],
        scratch_shapes=[
            pltpu.VMEM((2, 3 * HD, HD), F32), pltpu.VMEM((nz, 3 * HD, HD), F32),
            pltpu.VMEM((nx, 3 * HD, HD), F32),
            pltpu.VMEM((nz + 1, HD, 2 * HD), F32), pltpu.VMEM((nz + 1, HD, 2 * HD), F32),
            pltpu.VMEM((nx + 1, HD, HD), F32), pltpu.VMEM((nx + 1, HD, HD), F32),
            pltpu.VMEM((2, 2 * HD, HD), F32),
            dma, dma, dma((2, nz // 2)), dma((2, nz // 2)), dma((nx - 1,)), dma((nx - 1,)), dma, dma,
        ],
        compiler_params=pltpu.CompilerParams(collective_id=0, has_side_effects=True), name="scan",
    )(maps)
    dq, dk, dv, d_beta, d_lg = pl.pallas_call(
        grads_kernel,
        out_shape=(
            sd(q.shape, BF16), sd(q.shape, BF16), sd(q.shape, BF16), sd(beta.shape, F32), sd(beta.shape, F32),
        ),
        in_specs=vmem(10), out_specs=tuple(vmem(5)), name="grads",
    )(q, k, v, do, beta, lg, inverse, uw, back, sz)
    feats, cols = layer_input.shape[1], v.shape[1]
    piece = feats // nx
    dw = pl.pallas_call(
        lambda *refs: weight_kernel(nx, nz, *refs),
        out_shape=sd((feats * nz, cols), BF16),
        in_specs=vmem(2), out_specs=vmem(1)[0],
        scratch_shapes=[
            pltpu.VMEM((nz, T, cols), BF16), pltpu.VMEM((nx, piece, cols), BF16),
            pltpu.VMEM((nx, piece, cols), BF16), pltpu.VMEM((2, piece, cols), BF16),
            dma((2, nz // 2)), dma((2, nz // 2)), dma((nx - 1,)), dma((nx - 1,)), dma, dma,
            dma((nx - 1,)), dma((nx - 1,)), dma((2, nz // 2)), dma((2, nz // 2)),
        ],
        compiler_params=pltpu.CompilerParams(collective_id=1, has_side_effects=True), name="weight",
    )(dv, xg)
    return dq, dk, dv, d_beta, d_lg, dw


def solution(mesh):
    nz = mesh.shape["head"]
    nx = mesh.shape["seq"] // (nz * NY)
    split = P("seq", "head")
    return jax.shard_map(
        lambda *args: shards(nx, nz, *args),
        mesh=mesh, in_specs=(split,) * 7, out_specs=(split,) * 5 + (P(None, "head"),),
        check_vma=False,
    )
```

time: 1520 us -> 182 us (0.12)
  the two profiles are of different devices: /device:TPU:52 before, /device:TPU:64 now
where the time goes in v1:
time: 182 us
  Pallas kernels  152 us (84%)
  between operations  14.1 us (8%)
  local copies, waits for them, and re-layouts  9.45 us (5%)
  waiting for transfers between devices  4.59 us (3%)
  starting transfers between devices  1.96 us (1%)
    pallas_call x1, Pallas kernels, shards(): pl.pallas_call(lambda *refs: scan_kernel(nx, nz, *refs), out_shape=sd((2,...  78.2 us
    pallas_call x1, Pallas kernels, shards(): pl.pallas_call(lambda *refs: weight_kernel(nx, nz, *refs), out_shape=sd((...  61.2 us
    unnamed x7, local copies, waits for them, and re-layouts  9.45 us
    pallas_call x1, Pallas kernels, shards(): pl.pallas_call(maps_kernel, out_shape=(sd((2, 3 * HD, HD), F32), sd((2, T...  7.42 us
    pallas_call x1, Pallas kernels, shards(): pl.pallas_call(grads_kernel, out_shape=(sd(q.shape, BF16), sd(q.shape, BF...  4.71 us
    ppermute x1, waiting for transfers between devices, shards(): moved = lax.ppermute(layer_input, ('seq', 'head'), ranks)  4.57 us
  transfers between devices with their start and end apart: 2, of which 1 were waited for; matrix products, arithmetic and copies ran while one was open for 3% of the time, Pallas kernels for 50%

profile of v1, /device:TPU:64, one launch (start us, length us, event | category | flops | bytes accessed | tf_op | source)
XLA Modules:
  0.0 181.6 jit_solution(7912167337782494816)
XLA Ops:
  7.2 0.0 all-gather.2.cloned.1.call-start
  7.2 1.9 %collective-permute-start = (bf16[128,512]{1,0:T(8,128)(2,1)}, bf16[128,512]{1,0:T(8,128)(2,1)S(1)}, u32[]{:S(2)}, u32[]{:S(2)}) collective-permute-start(bf16[128,512]{1,0:T(8,128)(2,1)} %param.7), channel_id=1, source_target_pairs={{0,0},{1,16},{2,32},{3,48},{4,64},{5,80},{6,96},{7,112},{8,8},{9,2... | collective-permute-start | bytes 393224 | tf_op jit(solution)/shard_map/ppermute | solution.py:346
  9.1 4.6 %collective-permute-done = bf16[128,512]{1,0:T(8,128)(2,1)S(1)} collective-permute-done((bf16[128,512]{1,0:T(8,128)(2,1)}, bf16[128,512]{1,0:T(8,128)(2,1)S(1)}, u32[]{:S(2)}, u32[]{:S(2)}) %collective-permute-start) | collective-permute-done | bytes 131104 | tf_op jit(solution)/shard_map/ppermute | solution.py:346
  13.7 0.0 copy-start
  13.7 0.6 copy-done
  14.4 0.0 all-gather.2.cloned.1.call-update
  14.4 1.4 copy.15.beta
  15.8 1.4 copy.16.lg
  17.2 7.4 %maps.1 = (f32[2,384,128]{2,1,0:T(8,128)}, f32[2,128,128]{2,1,0:T(8,128)}, f32[2,128,256]{2,1,0:T(8,128)}, f32[2,128,128]{2,1,0:T(8,128)}) custom-call(bf16[128,256]{1,0:T(8,128)(2,1)} %q.3, bf16[128,256]{1,0:T(8,128)(2,1)} %k.3, bf16[128,256]{1,0:T(8,128)(2,1)} %v.3, bf16[128,256]{1,0:T(8,128)(2,1)} %do.3, f32[128,2]{1,0:T(8,128)} %copy.15.beta, ...), custom_call_target="tpu_custom_call" | custom-call | tf_op jit(solution)/shard_map/maps/pallas_call | solution.py:349
  24.6 78.2 %scan.1.sz = f32[2,256,128]{2,1,0:T(8,128)} custom-call(f32[2,384,128]{2,1,0:T(8,128)} %get-tuple-element.18.refs_0_), custom_call_target="tpu_custom_call" | custom-call | tf_op jit(solution)/shard_map/scan/pallas_call | solution.py:357
  102.8 4.7 %grads.1 = (bf16[128,256]{1,0:T(8,128)(2,1)}, bf16[128,256]{1,0:T(8,128)(2,1)}, bf16[128,256]{1,0:T(8,128)(2,1)}, f32[128,2]{1,0:T(8,128)}, f32[128,2]{1,0:T(8,128)}) custom-call(bf16[128,256]{1,0:T(8,128)(2,1)} %q.3, bf16[128,256]{1,0:T(8,128)(2,1)} %k.3, bf16[128,256]{1,0:T(8,128)(2,1)} %v.3, bf16[128,256]{1,0:T(8,128)(2,1)} %do.3, f32[128,2]{1,0:T(8,128)} %copy.15.beta, ...), custom_call_target="tpu_custom_call" | custom-call | tf_op jit(solution)/shard_map/grads/pallas_call | solution.py:371
  107.6 1.5 copy.17
  109.0 1.5 copy.18
  110.5 0.0 all-gather.2.cloned.1.call-done.refs_1_
  110.5 61.2 %weight.1 = bf16[4096,256]{1,0:T(8,128)(2,1)} custom-call(bf16[128,256]{1,0:T(8,128)(2,1)} %get-tuple-element.38.refs_0_, bf16[1024,512]{1,0:T(8,128)(2,1)} %all-gather.2.cloned.1.call-done.refs_1_), custom_call_target="tpu_custom_call" | custom-call | tf_op jit(solution)/shard_map/weight/pallas_call | solution.py:380
  171.7 3.0 %copy.20 = bf16[4096,256]{1,0:T(8,128)(2,1)} copy(bf16[4096,256]{1,0:T(8,128)(2,1)} %weight.1) | data formatting | bytes 4194304
Async XLA Ops:
  7.2 103.3 %all-gather.2.cloned.1.call-start = ((), (), s32[]{:S(2)}) async-start(), calls=%async_computation | async-start | bytes 1179648 | tf_op jit(solution)/shard_map/all_gather | solution.py:347
  7.2 6.5 %collective-permute-start = (bf16[128,512]{1,0:T(8,128)(2,1)}, bf16[128,512]{1,0:T(8,128)(2,1)S(1)}, u32[]{:S(2)}, u32[]{:S(2)}) collective-permute-start(bf16[128,512]{1,0:T(8,128)(2,1)} %param.7), channel_id=1, source_target_pairs={{0,0},{1,16},{2,32},{3,48},{4,64},{5,80},{6,96},{7,112},{8,8},{9,2... | collective-permute-start | bytes 393224 | tf_op jit(solution)/shard_map/ppermute | solution.py:346
  13.7 0.6 copy-start
Sparse Core Ops, SparseCore 0:
  14.5 56.2 all-gather.1

commit v2 on v1

v2 whole, which is shorter than its diff:
```python
import jax
import jax.numpy as jnp
from jax import lax
from jax.experimental import pallas as pl
from jax.experimental.pallas import tpu as pltpu
from jax.sharding import PartitionSpec as P

HD = 128
T = 128
F32 = jnp.float32
BF16 = jnp.bfloat16
HIGHEST = lax.Precision.HIGHEST
NY = 2


def dot(a, b, ca=1, cb=0):
    return lax.dot_general(
        a, b, (((ca,), (cb,)), ((), ())), precision=HIGHEST, preferred_element_type=F32
    )


def dot_exact(a, b, ca=1, cb=0):
    return lax.dot_general(a, b, (((ca,), (cb,)), ((), ())), preferred_element_type=F32)


def iotas():
    return (
        lax.broadcasted_iota(jnp.int32, (T, T), 0),
        lax.broadcasted_iota(jnp.int32, (T, T), 1),
    )


def unit_inverse(strict_lower):
    line, col = iotas()
    same = (line >= 64) == (col >= 64)
    diag_part = jnp.where(same, strict_lower, 0.0)
    below = jnp.where(same, 0.0, strict_lower)
    inverse = jnp.where(line == col, 1.0, 0.0) - diag_part
    power = dot(diag_part, diag_part)
    covered = 4
    while covered < 64:
        both = dot(jnp.concatenate([power, inverse], 0), power)
        inverse = inverse + both[T:]
        power = both[:T]
        covered = covered * 2
    inverse = inverse + dot(inverse, power)
    return inverse - dot(dot(inverse, below), inverse)


def as_column(row):
    line, col = iotas()
    return jnp.sum(jnp.where(line == col, row, 0.0), axis=1, keepdims=True)


def as_row(column):
    line, col = iotas()
    return jnp.sum(jnp.where(line == col, column, 0.0), axis=0, keepdims=True)


def gate_parts(lg_row):
    line, col = iotas()
    run_col = jnp.sum(jnp.where(col <= line, lg_row, 0.0), axis=1, keepdims=True)
    run_row = as_row(run_col)
    total = jnp.sum(lg_row, axis=1, keepdims=True)
    causal = line >= col
    decay = jnp.where(causal, jnp.exp(jnp.where(causal, run_col - run_row, 0.0)), 0.0)
    return decay, jnp.exp(run_col), jnp.exp(total - run_col), jnp.exp(total)


def local_maps(q, k, v, do, beta_row, lg_row):
    line, col = iotas()
    beta = as_column(beta_row)
    decay, growth, tail, keep = gate_parts(lg_row)
    keys = k.astype(F32)
    scores = decay * dot_exact(q, k, 1, 1)
    lower = beta * jnp.where(line > col, decay * dot_exact(k, k, 1, 1), 0.0)
    inverse = unit_inverse(lower)
    uw = dot(inverse, jnp.concatenate([beta * v.astype(F32), (beta * growth) * keys], 1))
    back = dot(scores, do.astype(F32), 0, 0)
    bw = dot(tail * keys, uw, 0, 0)
    eye = jnp.where(line == col, 1.0, 0.0)
    a = keep * eye - bw[:, HD:]
    b = bw[:, :HD]
    c = dot(growth * q.astype(F32), do.astype(F32), 0, 0) - dot(uw[:, HD:], back, 0, 0)
    return (a, b, c), (inverse, uw, back)


def local_grads(q, k, v, do, beta_row, lg_row, inverse, uw, back, state, adj):
    line, col = iotas()
    beta = as_column(beta_row)
    decay, growth, tail, keep = gate_parts(lg_row)
    queries, keys, values, grads = (m.astype(F32) for m in (q, k, v, do))
    update = uw[:, :HD] - dot(uw[:, HD:], state)
    d_update = back + dot(tail * keys, adj)
    e = dot(inverse, d_update, 0, 0)
    de = jnp.concatenate([grads, e], 0)
    by_state = dot(de, state, 1, 1)
    by_update = dot(de, update, 1, 1)
    nz = dot(update, adj, 1, 1)
    y = decay * by_update[:T]
    xp = -jnp.where(line > col, decay * by_update[T:], 0.0)
    by_key = dot(jnp.concatenate([xp, y], 0), keys)
    r = by_key[:T] - growth * by_state[T:]
    crossed = dot(
        jnp.concatenate([beta * xp, y], 0), jnp.concatenate([keys, queries], 0), 0, 0
    )
    dq = growth * by_state[:T] + by_key[T:]
    tail_nz = tail * nz
    dk_col = crossed + tail_nz
    dk_row = beta * r
    dv = beta * e
    d_beta = jnp.sum(e * values + keys * r, axis=1, keepdims=True)
    d_run = jnp.sum(queries * dq + keys * (dk_row - dk_col), axis=1, keepdims=True)
    last = jnp.sum(tail_nz * keys, axis=(0, 1), keepdims=True) + keep * jnp.sum(
        adj * state, axis=(0, 1), keepdims=True
    )
    d_lg = jnp.sum(jnp.where(line >= col, d_run, 0.0), axis=0, keepdims=True) + last
    return dq, dk_row + dk_col, dv, as_row(d_beta), d_lg


class Place:
    def __init__(self, nx, nz):
        s = lax.axis_index("seq")
        self.nx, self.nz = nx, nz
        self.x = s // (nz * NY)
        self.z = lax.rem(s // NY, nz)
        self.y = lax.rem(s, NY)
        self.h = lax.axis_index("head")

    def at(self, x=None, z=None, y=None):
        x = self.x if x is None else x
        z = self.z if z is None else z
        y = self.y if y is None else y
        return {"seq": (x * self.nz + z) * NY + y}

    def partner(self):
        return self.at(y=1 - self.y)

    def along_z(self, t):
        return self.at(z=lax.rem(self.z + t, self.nz))

    def other_x(self, t):
        return lax.rem(self.x + t, self.nx)

    def along_head(self, t):
        return {"head": lax.rem(self.h + t, self.nz)}

    def swap_to(self):
        return {**self.at(z=lax.rem(self.h + self.nz - 1, self.nz)), "head": self.z}

    def swap_from(self):
        return {**self.at(z=self.h), "head": lax.rem(self.z + 1, self.nz)}

    def greet(self):
        barrier = pltpu.get_barrier_semaphore()
        peers = [self.partner(), self.swap_to(), self.swap_from()]
        peers += [self.along_z(t) for t in range(1, self.nz)]
        peers += [self.along_head(t) for t in range(1, self.nz)]
        peers += [self.at(x=self.other_x(t)) for t in range(1, self.nx)]
        for peer in peers:
            pl.semaphore_signal(
                barrier, inc=1, device_id=peer, device_id_type=pl.DeviceIdType.MESH
            )
        pl.semaphore_wait(barrier, len(peers))


def remote(src, dst, sems, device):
    return pltpu.make_async_remote_copy(
        src_ref=src, dst_ref=dst, send_sem=sems[0], recv_sem=sems[1],
        device_id=device, device_id_type=pl.DeviceIdType.MESH,
    )


def begin(copies, sent):
    for copy in copies:
        copy.start()
    sent += copies
    return copies


def arrive(copies):
    for copy in copies:
        copy.wait_recv()


def ring_z(place, view, sems, sent):
    nz, z = place.nz, place.z
    steps = nz // 2
    before = [None, None]
    for t in range(1, steps + 1):
        for way, away, ahead in ((0, nz - t + 1, 1), (1, t - 1, nz - 1)):
            src = view(lax.rem(z + away, nz), way if t == steps else None)
            if before[way] is not None:
                before[way].wait_recv()
            copy = remote(src, src, sems(way, t - 1), place.along_z(ahead))
            copy.start()
            sent.append(copy)
            before[way] = copy
        yield t
    arrive(before)


def compose(out, later, earlier):
    a, below = later[0:HD], earlier[0:HD]
    ab = dot(a, jnp.concatenate([below, earlier[HD : 2 * HD]], 1))
    c = earlier[2 * HD : 3 * HD] + dot(below, later[2 * HD : 3 * HD], 0, 0)
    b = ab[:, HD:] + later[HD : 2 * HD]
    out[0:HD] = ab[:, :HD]
    out[HD : 2 * HD] = b
    out[2 * HD : 3 * HD] = c


def chains(blocks, count, forth, aback):
    def step(n, carry):
        m = count - 1 - n
        forth[n + 1] = dot(blocks[n, 0:HD], forth[n]) + blocks[n, HD : 2 * HD]
        aback[m] = dot(blocks[m, 0:HD], aback[m + 1], 0, 0) + blocks[m, 2 * HD : 3 * HD]
        return carry

    lax.fori_loop(0, count, step, 0)


def layer_kernel(
    nx, nz, li, q, k, v, do, beta, lg, dq, dk, dv, d_beta, d_lg, dw,
    theirs, their_gates, xg, inverse, uw, back, pair, zbuf, left, right, joined, xbuf, xf, xb, both,
    ret, ret_gate, got_gate, g, psend, precv, ybuf, *sem_refs
):
    in_s, sw_s, hd_s, z_s, x_s, ret_s, g_s, p_s, y_s, ax_s, az_s = (
        (lambda a, b: lambda *i: (a.at[i], b.at[i]))(sem_refs[2 * n], sem_refs[2 * n + 1])
        for n in range(11)
    )
    place = Place(nx, nz)
    x, z, y, h = place.x, place.z, place.y, place.h
    mine = pl.ds(pl.multiple_of(y * HD, HD), HD)
    yours = pl.ds(pl.multiple_of((1 - y) * HD, HD), HD)
    sent = []
    place.greet()

    asked = [
        remote(ref.at[:, yours], theirs.at[n], in_s(n), place.partner())
        for n, ref in enumerate((q, k, v, do))
    ]
    asked += [
        remote(ref, their_gates.at[n], in_s(4 + n), place.partner())
        for n, ref in enumerate((beta, lg))
    ]
    begin(asked, sent)
    swapped = begin([remote(li, xg.at[z], sw_s(0), place.swap_to())], sent)

    line, col = iotas()
    zero = jnp.zeros((HD, HD), F32)
    for ref in (left, right):
        for n in range(2):
            ref[n, 0:HD] = jnp.where(line == col, 1.0, 0.0)
            ref[n, HD : 2 * HD] = zero
            ref[n, 2 * HD : 3 * HD] = zero
    xf[0] = zero
    xb[nx] = zero
    ret_gate[...] = jnp.zeros_like(ret_gate)

    def inputs(n):
        if n == 0:
            parts = [ref[:, mine] for ref in (q, k, v, do)]
            return parts + [beta[pl.ds(y, 1), :], lg[pl.ds(y, 1), :]]
        parts = [theirs[i] for i in range(4)]
        return parts + [their_gates[i, pl.ds(y, 1), :] for i in range(2)]

    for n in range(2):
        if n == 1:
            arrive(asked)
        (a, b, c), (inv, u, f) = local_maps(*inputs(n))
        slot = y if n == 0 else 1 - y
        pair[slot, 0:HD] = a
        pair[slot, HD : 2 * HD] = b
        pair[slot, 2 * HD : 3 * HD] = c
        inverse[n] = inv
        uw[n] = u
        back[n] = f

    compose(zbuf.at[z], pair.at[1], pair.at[0])
    part_rows = 3 * HD // 2

    def zview(slot, part):
        return zbuf.at[slot] if part is None else zbuf.at[slot, pl.ds(part * part_rows, part_rows)]

    def fold(t):
        wrapped = (z < t).astype(jnp.int32)
        acc = left.at[wrapped]
        compose(acc, acc, zbuf.at[lax.rem(z + nz - t, nz)])
        if t < nz // 2:
            wrapped = (z + t >= nz).astype(jnp.int32)
            acc = right.at[wrapped]
            compose(acc, zbuf.at[lax.rem(z + t, nz)], acc)

    for t in ring_z(place, zview, z_s, sent):
        if t == 1:
            arrive(swapped)
            spread = begin(
                [
                    remote(xg.at[h], xg.at[h], hd_s(n - 1), place.along_head(n))
                    for n in range(1, nz)
                ],
                sent,
            )
        else:
            fold(t - 1)
    fold(nz // 2)
    compose(joined.at[0], left.at[0], right.at[1])
    compose(joined.at[1], left.at[1], right.at[0])
    compose(joined.at[2], zbuf.at[z], joined.at[0])
    compose(xbuf.at[x], joined.at[1], joined.at[2])
    totals = begin(
        [
            remote(xbuf.at[x], xbuf.at[x], x_s(t - 1), place.at(x=place.other_x(t)))
            for t in range(1, nx)
        ],
        sent,
    )
    arrive(totals)
    chains(xbuf, nx, xf, xb)
    state = dot(joined[0, 0:HD], xf[x]) + joined[0, HD : 2 * HD]
    adj = dot(joined[1, 0:HD], xb[x + 1], 0, 0) + joined[1, 2 * HD : 3 * HD]
    both[0, 0:HD] = state
    both[0, HD : 2 * HD] = dot(pair[1, 0:HD], adj, 0, 0) + pair[1, 2 * HD : 3 * HD]
    both[1, 0:HD] = dot(pair[0, 0:HD], state) + pair[0, HD : 2 * HD]
    both[1, HD : 2 * HD] = adj

    def grads(n):
        slot = y if n == 0 else 1 - y
        return local_grads(
            *inputs(n), inverse[n], uw[n], back[n], both[slot, 0:HD], both[slot, HD : 2 * HD]
        )

    gq, gk, gv, gb, gl = grads(1)
    ret[2] = gv.astype(BF16)
    given = begin([remote(ret.at[2], g.at[1, z], ret_s(2), place.partner())], sent)
    ret[0] = gq.astype(BF16)
    ret[1] = gk.astype(BF16)
    ret_gate[0:1] = gb
    ret_gate[1:2] = gl
    returned = begin(
        [
            remote(ret.at[0], dq.at[:, mine], ret_s(0), place.partner()),
            remote(ret.at[1], dk.at[:, mine], ret_s(1), place.partner()),
            remote(ret_gate, got_gate, ret_s(3), place.partner()),
        ],
        sent,
    )
    gq, gk, gv, gb, gl = grads(0)
    g[0, z] = gv.astype(BF16)

    def share(p):
        return begin(
            [
                remote(g.at[p, z], g.at[p, z], g_s(p, t - 1), place.along_z(t))
                for t in range(1, nz)
            ],
            sent,
        )

    shared = [share(0)]
    arrive(given)
    shared.append(share(1))
    dq[:, mine] = gq.astype(BF16)
    dk[:, mine] = gk.astype(BF16)
    dv[:, mine] = gv.astype(BF16)
    dv[:, yours] = g[1, z]
    d_beta[pl.ds(y, 1), :] = gb
    d_lg[pl.ds(y, 1), :] = gl

    arrive(spread)
    feats = xg[...].reshape(nz * T, xg.shape[2])
    scattered = []
    for p in range(2):
        arrive(shared[p])
        total = dot_exact(g[p].reshape(nz * T, HD), feats, 0, 0)
        for n in range(nx):
            psend[p, n] = total[:, n * HD : (n + 1) * HD].astype(BF16)
        scattered.append(
            begin(
                [
                    remote(
                        psend.at[p, place.other_x(t)], precv.at[p, x], p_s(p, t - 1),
                        place.at(x=place.other_x(t)),
                    )
                    for t in range(1, nx)
                ],
                sent,
            )
        )
        precv[p, x] = psend[p, x]
    over = []
    for p in range(2):
        arrive(scattered[p])
        total = precv[p, 0].astype(F32)
        for n in range(1, nx):
            total = total + precv[p, n].astype(F32)
        who = y if p == 0 else 1 - y
        ybuf[who, y] = total.astype(BF16)
        over += begin(
            [remote(ybuf.at[who, y], ybuf.at[who, y], y_s(p), place.partner())], sent
        )

    def chunk(slot):
        return lax.rem(slot + 1, nz)

    arrive(over)
    for p in range(2):
        total = ybuf[p, 0].astype(F32) + ybuf[p, 1].astype(F32)
        dw[p, chunk(z), x] = total.T.astype(BF16)
    one, two = y, 1 - y
    half = nx // 2
    by_x = begin(
        [
            remote(
                dw.at[one, chunk(z), x], dw.at[one, chunk(z), x], ax_s(0, t - 1),
                place.at(x=place.other_x(t)),
            )
            for t in range(1, nx)
        ],
        sent,
    )

    def view_wide(slot, part):
        if part is None:
            return dw.at[one, chunk(slot)]
        return dw.at[one, chunk(slot), pl.ds(part * half, half)]

    def view_narrow(slot, part):
        if part is None:
            return dw.at[two, chunk(slot), x]
        return dw.at[two, chunk(slot), x, pl.ds(part * (HD // 2), HD // 2)]

    narrow = ring_z(place, view_narrow, lambda *i: az_s(1, *i), sent)
    wide = ring_z(place, view_wide, lambda *i: az_s(0, *i), sent)
    next(narrow)
    arrive(by_x)
    next(wide)
    for _ in narrow:
        next(wide)
    by_x = begin(
        [
            remote(dw.at[two, :, x], dw.at[two, :, x], ax_s(1, t - 1), place.at(x=place.other_x(t)))
            for t in range(1, nx)
        ],
        sent,
    )
    for _ in wide:
        pass
    arrive(returned)
    d_beta[pl.ds(1 - y, 1), :] = got_gate[0:1]
    d_lg[pl.ds(1 - y, 1), :] = got_gate[1:2]
    arrive(by_x)
    for copy in sent:
        copy.wait_send()


def finish_kernel(*refs):
    ins, outs = refs[:6], refs[6:]
    for src, dst in zip(ins[:5], outs[:5]):
        dst[...] = src[...]
    heads, nz, nx = ins[5].shape[:3]
    for c in range(nz):
        for n in range(nx):
            for p in range(heads):
                rows = pl.ds((c * nx + n) * HD, HD)
                outs[5][rows, p * HD : (p + 1) * HD] = ins[5][p, c, n]


def vmem(count):
    return [pl.BlockSpec(memory_space=pltpu.VMEM)] * count


def shards(nx, nz, layer_input, q, k, v, beta, lg, do):
    sd = jax.ShapeDtypeStruct
    rows = sd((2, T), F32)
    wide = sd(q.shape, BF16)
    scratch = pltpu.VMEM
    sems = [
        (6,), (1,), (nz - 1,), (2, nz // 2), (nx - 1,), (4,), (2, nz - 1), (2, nx - 1), (2,),
        (2, nx - 1), (2, 2, nz // 2),
    ]
    outs = pl.pallas_call(
        lambda *refs: layer_kernel(nx, nz, *refs),
        out_shape=(wide, wide, wide, rows, rows, sd((2, nz, nx, HD, HD), BF16)),
        in_specs=vmem(7), out_specs=tuple(vmem(6)),
        scratch_shapes=[
            scratch((4, T, HD), BF16), scratch((2, 2, T), F32),
            scratch((nz, T, layer_input.shape[1]), BF16),
            scratch((2, T, T), F32), scratch((2, T, 2 * HD), F32), scratch((2, T, HD), F32),
            scratch((2, 3 * HD, HD), F32), scratch((nz, 3 * HD, HD), F32),
            scratch((2, 3 * HD, HD), F32), scratch((2, 3 * HD, HD), F32), scratch((3, 3 * HD, HD), F32),
            scratch((nx, 3 * HD, HD), F32), scratch((nx + 1, HD, HD), F32), scratch((nx + 1, HD, HD), F32),
            scratch((2, 2 * HD, HD), F32),
            scratch((3, T, HD), BF16), scratch((8, T), F32), scratch((8, T), F32),
            scratch((2, nz, T, HD), BF16), scratch((2, nx, HD, HD), BF16), scratch((2, nx, HD, HD), BF16),
            scratch((2, 2, HD, HD), BF16),
        ]
        + [pltpu.SemaphoreType.DMA(shape) for shape in sems for _ in range(2)],
        compiler_params=pltpu.CompilerParams(
            collective_id=0, has_side_effects=True, vmem_limit_bytes=48 * 2**20
        ),
        name="layer",
    )(layer_input, q, k, v, do, beta.T, lg.T)
    dq, dk, dv, d_beta, d_lg, dw = pl.pallas_call(
        finish_kernel,
        out_shape=(wide, wide, wide, rows, rows, sd((nz * nx * HD, v.shape[1]), BF16)),
        in_specs=vmem(6), out_specs=tuple(vmem(6)), name="finish",
    )(*outs)
    return dq, dk, dv, d_beta.T, d_lg.T, dw


def solution(mesh):
    nz = mesh.shape["head"]
    nx = mesh.shape["seq"] // (nz * NY)
    split = P("seq", "head")
    return jax.shard_map(
        lambda *args: shards(nx, nz, *args),
        mesh=mesh, in_specs=(split,) * 7, out_specs=(split,) * 5 + (P(None, "head"),),
        check_vma=False,
    )
```

time: 182 us -> 129 us (0.71)
  the two profiles are of different devices: /device:TPU:64 before, /device:TPU:24 now
where the time goes in v2:
time: 129 us; the launch traced here: 128 us
  Pallas kernels  118 us (91%)
  local copies, waits for them, and re-layouts  9.88 us (8%)
    pallas_call x1, Pallas kernels, shards(): pl.pallas_call(lambda *refs: layer_kernel(nx, nz, *refs), out_shape=(wide...  114 us
    unnamed x26, local copies, waits for them, and re-layouts  9.88 us
    pallas_call x1, Pallas kernels, shards(): pl.pallas_call(finish_kernel, out_shape=(wide, wide, wide, rows, rows, sd...  3.44 us

profile of v2, /device:TPU:24, one launch (start us, length us, event | category | flops | bytes accessed | tf_op | source)
XLA Modules:
  0.0 128.3 jit_solution(7587224027042179994)
XLA Ops:
  0.6 0.0 copy-start.1
  0.6 0.9 copy-done.1
  1.5 0.0 copy-start.2
  1.5 0.8 copy-done.2
  2.4 0.8 copy-done.3
  3.2 0.8 copy-done.4
  4.1 0.8 copy-done.5
  4.9 0.7 copy-done.9
  5.6 0.0 copy-start.10
  5.6 0.7 copy-done.10
  6.3 114.3 %layer.1 = (bf16[128,256]{1,0:T(8,128)(2,1)S(1)}, bf16[128,256]{1,0:T(8,128)(2,1)S(1)}, bf16[128,256]{1,0:T(8,128)(2,1)S(1)}, f32[2,128]{1,0:T(2,128)S(1)}, f32[...) custom-call(bf16[128,512]{1,0:T(8,128)(2,1)S(1)} %copy-done.1, bf16[128,256]{1,0:T(8,128)(2,1)S(1)} %copy-done.2, ...), custom_call_target="tpu_custom_call" | custom-call | tf_op jit(solution)/shard_map/layer/pallas_call | solution.py:483
  120.6 0.0 copy-start
  120.6 1.3 %copy-done = bf16[2,8,4,128,128]{4,3,2,1,0:T(8,128)(2,1)} copy-done((bf16[2,8,4,128,128]{4,3,2,1,0:T(8,128)(2,1)}, bf16[2,8,4,128,128]{4,3,2,1,0:T(8,128)(2,1)S(1)}, u32[]{:S(2)}) %copy-start) | copy-done | bytes 2097176
  121.9 0.0 copy-start.6
  121.9 0.6 copy-done.6
  122.6 0.0 copy-start.7
  122.6 0.6 copy-done.7
  123.2 0.0 copy-start.8
  123.2 0.6 copy-done.8
  123.8 0.0 copy-start.11
  123.8 0.5 copy-done.11
  124.3 0.0 copy-start.12
  124.3 0.5 copy-done.12
  124.9 3.4 %finish.1 = (bf16[128,256]{1,0:T(8,128)(2,1)}, bf16[128,256]{1,0:T(8,128)(2,1)}, bf16[128,256]{1,0:T(8,128)(2,1)}, f32[2,128]{1,0:T(2,128)}, f32[2,128]{1,0:T(2,128)}, /*index=5*/bf16[4096,256]{1,0:T(8,128)(2,1)}) custom-call(bf16[128,256]{1,0:T(8,128)(2,1)} %copy-done.6, bf16[128,256]{1,0:T(8,128)(2,1)} %copy-done.7, bf16[128,256]{1,0:T(8,128)(2,1)} %copy-done.8, ...), custom_call_target="tpu_custom_call" | custom-call | tf_op jit(solution)/shard_map/finish/pallas_call | solution.py:505
  (4 shorter events, 0.0 us)
Async XLA Ops:
  0.6 0.9 copy-start.1
  1.5 0.8 copy-start.2
  2.4 0.8 copy-start.3
  3.2 0.8 copy-start.4
  4.1 0.8 copy-start.5
  4.9 0.7 copy-start.9
  5.6 0.7 copy-start.10
  120.6 1.3 %copy-start = (bf16[2,8,4,128,128]{4,3,2,1,0:T(8,128)(2,1)}, bf16[2,8,4,128,128]{4,3,2,1,0:T(8,128)(2,1)S(1)}, u32[]{:S(2)}) copy-start(bf16[2,8,4,128,128]{4,3,2,1,0:T(8,128)(2,1)S(1)} %get-tuple-element.23.refs_5_) | copy-start | bytes 6291460
  121.9 0.6 copy-start.6
  122.6 0.6 copy-start.7
  123.2 0.6 copy-start.8
  123.8 0.5 copy-start.11
  124.3 0.5 copy-start.12

commit v3 on v2

--- a/solution.py
+++ b/solution.py
@@ -186,35 +186,41 @@
 def ring_z(place, view, sems, sent):
     nz, z = place.nz, place.z
     steps = nz // 2
-    before = [None, None]
+    before = {}
     for t in range(1, steps + 1):
-        for way, away, ahead in ((0, nz - t + 1, 1), (1, t - 1, nz - 1)):
-            src = view(lax.rem(z + away, nz), way if t == steps else None)
-            if before[way] is not None:
-                before[way].wait_recv()
-            copy = remote(src, src, sems(way, t - 1), place.along_z(ahead))
-            copy.start()
-            sent.append(copy)
-            before[way] = copy
+        for part in range(2):
+            for way, away, ahead in ((0, nz - t + 1, 1), (1, t - 1, nz - 1)):
+                if (way, part) in before:
+                    before.pop((way, part)).wait_recv()
+                if t == steps and part != way:
+                    continue
+                src = view(lax.rem(z + away, nz), part)
+                copy = remote(src, src, sems(way, part, t - 1), place.along_z(ahead))
+                copy.start()
+                sent.append(copy)
+                before[way, part] = copy
         yield t
-    arrive(before)
+    arrive(before.values())
+
+
+OFFSET, MAP, ADJ = slice(0, HD), slice(HD, 2 * HD), slice(2 * HD, 3 * HD)
 
 
 def compose(out, later, earlier):
-    a, below = later[0:HD], earlier[0:HD]
-    ab = dot(a, jnp.concatenate([below, earlier[HD : 2 * HD]], 1))
-    c = earlier[2 * HD : 3 * HD] + dot(below, later[2 * HD : 3 * HD], 0, 0)
-    b = ab[:, HD:] + later[HD : 2 * HD]
-    out[0:HD] = ab[:, :HD]
-    out[HD : 2 * HD] = b
-    out[2 * HD : 3 * HD] = c
+    a, below = later[MAP], earlier[MAP]
+    ab = dot(a, jnp.concatenate([below, earlier[OFFSET]], 1))
+    c = earlier[ADJ] + dot(below, later[ADJ], 0, 0)
+    b = ab[:, HD:] + later[OFFSET]
+    out[MAP] = ab[:, :HD]
+    out[OFFSET] = b
+    out[ADJ] = c
 
 
 def chains(blocks, count, forth, aback):
     def step(n, carry):
         m = count - 1 - n
-        forth[n + 1] = dot(blocks[n, 0:HD], forth[n]) + blocks[n, HD : 2 * HD]
-        aback[m] = dot(blocks[m, 0:HD], aback[m + 1], 0, 0) + blocks[m, 2 * HD : 3 * HD]
+        forth[n + 1] = dot(blocks[n, MAP], forth[n]) + blocks[n, OFFSET]
+        aback[m] = dot(blocks[m, MAP], aback[m + 1], 0, 0) + blocks[m, ADJ]
         return carry
 
     lax.fori_loop(0, count, step, 0)
@@ -222,26 +228,36 @@
 
 def layer_kernel(
     nx, nz, li, q, k, v, do, beta, lg, dq, dk, dv, d_beta, d_lg, dw,
-    theirs, their_gates, xg, inverse, uw, back, pair, zbuf, left, right, joined, xbuf, xf, xb, both,
-    ret, ret_gate, got_gate, g, psend, precv, ybuf, *sem_refs
+    inp, gates, xg, inverse, uw, back, pair, zbuf, left, right, joined, xbuf, xf, xb, both,
+    ret, ret_gate, got_gate, g, psend, precv, ybuf, load_sems, *sem_refs
 ):
-    in_s, sw_s, hd_s, z_s, x_s, ret_s, g_s, p_s, y_s, ax_s, az_s = (
+    in_s, sw_s, hd_s, z_s, x_s, ret_s, g_s, p_s, y_s, ax_s, an_s, az_s = (
         (lambda a, b: lambda *i: (a.at[i], b.at[i]))(sem_refs[2 * n], sem_refs[2 * n + 1])
-        for n in range(11)
+        for n in range(12)
     )
     place = Place(nx, nz)
     x, z, y, h = place.x, place.z, place.y, place.h
     mine = pl.ds(pl.multiple_of(y * HD, HD), HD)
     yours = pl.ds(pl.multiple_of((1 - y) * HD, HD), HD)
     sent = []
+    loads = [
+        pltpu.make_async_copy(ref.at[:, mine], inp.at[0, n], load_sems.at[n])
+        for n, ref in enumerate((q, k, v, do))
+    ]
+    loads += [
+        pltpu.make_async_copy(ref, gates.at[0, n], load_sems.at[4 + n])
+        for n, ref in enumerate((beta, lg))
+    ]
+    for load in loads:
+        load.start()
     place.greet()
 
     asked = [
-        remote(ref.at[:, yours], theirs.at[n], in_s(n), place.partner())
+        remote(ref.at[:, yours], inp.at[1, n], in_s(n), place.partner())
         for n, ref in enumerate((q, k, v, do))
     ]
     asked += [
-        remote(ref, their_gates.at[n], in_s(4 + n), place.partner())
+        remote(ref, gates.at[1, n], in_s(4 + n), place.partner())
         for n, ref in enumerate((beta, lg))
     ]
     begin(asked, sent)
@@ -251,37 +267,39 @@
     zero = jnp.zeros((HD, HD), F32)
     for ref in (left, right):
         for n in range(2):
-            ref[n, 0:HD] = jnp.where(line == col, 1.0, 0.0)
-            ref[n, HD : 2 * HD] = zero
-            ref[n, 2 * HD : 3 * HD] = zero
+            ref[n, MAP] = jnp.where(line == col, 1.0, 0.0)
+            ref[n, OFFSET] = zero
+            ref[n, ADJ] = zero
     xf[0] = zero
     xb[nx] = zero
     ret_gate[...] = jnp.zeros_like(ret_gate)
+    for load in loads:
+        load.wait()
 
     def inputs(n):
-        if n == 0:
-            parts = [ref[:, mine] for ref in (q, k, v, do)]
-            return parts + [beta[pl.ds(y, 1), :], lg[pl.ds(y, 1), :]]
-        parts = [theirs[i] for i in range(4)]
-        return parts + [their_gates[i, pl.ds(y, 1), :] for i in range(2)]
-
-    for n in range(2):
-        if n == 1:
+        return [inp[n, i] for i in range(4)] + [gates[n, i, pl.ds(y, 1), :] for i in range(2)]
+
+    def maps_of(n, carry):
+        @pl.when(n == 1)
+        def _():
             arrive(asked)
+
         (a, b, c), (inv, u, f) = local_maps(*inputs(n))
-        slot = y if n == 0 else 1 - y
-        pair[slot, 0:HD] = a
-        pair[slot, HD : 2 * HD] = b
-        pair[slot, 2 * HD : 3 * HD] = c
+        slot = lax.rem(y + n, 2)
+        pair[slot, MAP] = a
+        pair[slot, OFFSET] = b
+        pair[slot, ADJ] = c
         inverse[n] = inv
         uw[n] = u
         back[n] = f
-
+        return carry
+
+    lax.fori_loop(0, 2, maps_of, 0)
     compose(zbuf.at[z], pair.at[1], pair.at[0])
     part_rows = 3 * HD // 2
 
     def zview(slot, part):
-        return zbuf.at[slot] if part is None else zbuf.at[slot, pl.ds(part * part_rows, part_rows)]
+        return zbuf.at[slot, pl.ds(part * part_rows, part_rows)]
 
     def fold(t):
         wrapped = (z < t).astype(jnp.int32)
@@ -309,45 +327,51 @@
     compose(joined.at[1], left.at[1], right.at[0])
     compose(joined.at[2], zbuf.at[z], joined.at[0])
     compose(xbuf.at[x], joined.at[1], joined.at[2])
-    totals = begin(
-        [
-            remote(xbuf.at[x], xbuf.at[x], x_s(t - 1), place.at(x=place.other_x(t)))
-            for t in range(1, nx)
-        ],
-        sent,
-    )
+    totals = []
+    for t in range(1, nx):
+        other = place.other_x(t)
+        low = jnp.where(other > x, 0, HD)
+        rows = xbuf.at[x, pl.ds(pl.multiple_of(low, HD), 2 * HD)]
+        totals.append(remote(rows, rows, x_s(t - 1), place.at(x=other)))
+    begin(totals, sent)
     arrive(totals)
     chains(xbuf, nx, xf, xb)
-    state = dot(joined[0, 0:HD], xf[x]) + joined[0, HD : 2 * HD]
-    adj = dot(joined[1, 0:HD], xb[x + 1], 0, 0) + joined[1, 2 * HD : 3 * HD]
-    both[0, 0:HD] = state
-    both[0, HD : 2 * HD] = dot(pair[1, 0:HD], adj, 0, 0) + pair[1, 2 * HD : 3 * HD]
-    both[1, 0:HD] = dot(pair[0, 0:HD], state) + pair[0, HD : 2 * HD]
-    both[1, HD : 2 * HD] = adj
-
-    def grads(n):
-        slot = y if n == 0 else 1 - y
-        return local_grads(
-            *inputs(n), inverse[n], uw[n], back[n], both[slot, 0:HD], both[slot, HD : 2 * HD]
+    state = dot(joined[0, MAP], xf[x]) + joined[0, OFFSET]
+    adj = dot(joined[1, MAP], xb[x + 1], 0, 0) + joined[1, ADJ]
+    both[0, 0] = state
+    both[0, 1] = dot(pair[1, MAP], adj, 0, 0) + pair[1, ADJ]
+    both[1, 0] = dot(pair[0, MAP], state) + pair[0, OFFSET]
+    both[1, 1] = adj
+
+    given = [remote(ret.at[1, 2], g.at[1, z], ret_s(2), place.partner())]
+    returned = [
+        remote(ret.at[1, 0], dq.at[:, mine], ret_s(0), place.partner()),
+        remote(ret.at[1, 1], dk.at[:, mine], ret_s(1), place.partner()),
+        remote(ret_gate.at[1], got_gate, ret_s(3), place.partner()),
+    ]
+
+    def grads_of(turn, carry):
+        n = 1 - turn
+        slot = lax.rem(y + n, 2)
+        gq, gk, gv, gb, gl = local_grads(
+            *inputs(n), inverse[n], uw[n], back[n], both[slot, 0], both[slot, 1]
         )
-
-    gq, gk, gv, gb, gl = grads(1)
-    ret[2] = gv.astype(BF16)
-    given = begin([remote(ret.at[2], g.at[1, z], ret_s(2), place.partner())], sent)
-    ret[0] = gq.astype(BF16)
-    ret[1] = gk.astype(BF16)
-    ret_gate[0:1] = gb
-    ret_gate[1:2] = gl
-    returned = begin(
-        [
-            remote(ret.at[0], dq.at[:, mine], ret_s(0), place.partner()),
-            remote(ret.at[1], dk.at[:, mine], ret_s(1), place.partner()),
-            remote(ret_gate, got_gate, ret_s(3), place.partner()),
-        ],
-        sent,
-    )
-    gq, gk, gv, gb, gl = grads(0)
-    g[0, z] = gv.astype(BF16)
+        ret[n, 0] = gq.astype(BF16)
+        ret[n, 1] = gk.astype(BF16)
+        ret[n, 2] = gv.astype(BF16)
+        ret_gate[n, 0:1] = gb
+        ret_gate[n, 1:2] = gl
+
+        @pl.when(turn == 0)
+        def _():
+            for copy in given + returned:
+                copy.start()
+
+        return carry
+
+    lax.fori_loop(0, 2, grads_of, 0)
+    sent += given + returned
+    g[0, z] = ret[0, 2]
 
     def share(p):
         return begin(
@@ -361,18 +385,18 @@
     shared = [share(0)]
     arrive(given)
     shared.append(share(1))
-    dq[:, mine] = gq.astype(BF16)
-    dk[:, mine] = gk.astype(BF16)
-    dv[:, mine] = gv.astype(BF16)
+    dq[:, mine] = ret[0, 0]
+    dk[:, mine] = ret[0, 1]
+    dv[:, mine] = ret[0, 2]
     dv[:, yours] = g[1, z]
-    d_beta[pl.ds(y, 1), :] = gb
-    d_lg[pl.ds(y, 1), :] = gl
+    d_beta[pl.ds(y, 1), :] = ret_gate[0, 0:1]
+    d_lg[pl.ds(y, 1), :] = ret_gate[0, 1:2]
 
     arrive(spread)
-    feats = xg[...].reshape(nz * T, xg.shape[2])
     scattered = []
     for p in range(2):
         arrive(shared[p])
+        feats = xg[...].reshape(nz * T, xg.shape[2])
         total = dot_exact(g[p].reshape(nz * T, HD), feats, 0, 0)
         for n in range(nx):
             psend[p, n] = total[:, n * HD : (n + 1) * HD].astype(BF16)
@@ -408,41 +432,27 @@
     for p in range(2):
         total = ybuf[p, 0].astype(F32) + ybuf[p, 1].astype(F32)
         dw[p, chunk(z), x] = total.T.astype(BF16)
+
     one, two = y, 1 - y
+    piece = dw.at[one, chunk(z), x]
+    by_x = begin(
+        [remote(piece, piece, ax_s(0, t - 1), place.at(x=place.other_x(t))) for t in range(1, nx)],
+        sent,
+    )
+    piece = dw.at[two, chunk(z), x]
+    by_z = begin(
+        [remote(piece, piece, an_s(t - 1), place.along_z(t)) for t in range(1, nz)], sent
+    )
     half = nx // 2
-    by_x = begin(
-        [
-            remote(
-                dw.at[one, chunk(z), x], dw.at[one, chunk(z), x], ax_s(0, t - 1),
-                place.at(x=place.other_x(t)),
-            )
-            for t in range(1, nx)
-        ],
-        sent,
-    )
-
-    def view_wide(slot, part):
-        if part is None:
-            return dw.at[one, chunk(slot)]
-        return dw.at[one, chunk(slot), pl.ds(part * half, half)]
-
-    def view_narrow(slot, part):
-        if part is None:
-            return dw.at[two, chunk(slot), x]
-        return dw.at[two, chunk(slot), x, pl.ds(part * (HD // 2), HD // 2)]
-
-    narrow = ring_z(place, view_narrow, lambda *i: az_s(1, *i), sent)
-    wide = ring_z(place, view_wide, lambda *i: az_s(0, *i), sent)
-    next(narrow)
+    wide = ring_z(
+        place, lambda slot, part: dw.at[one, chunk(slot), pl.ds(part * half, half)], az_s, sent
+    )
     arrive(by_x)
     next(wide)
-    for _ in narrow:
-        next(wide)
+    arrive(by_z)
+    pieces = dw.at[two, :, x]
     by_x = begin(
-        [
-            remote(dw.at[two, :, x], dw.at[two, :, x], ax_s(1, t - 1), place.at(x=place.other_x(t)))
-            for t in range(1, nx)
-        ],
+        [remote(pieces, pieces, ax_s(1, t - 1), place.at(x=place.other_x(t))) for t in range(1, nx)],
         sent,
     )
     for _ in wide:
@@ -477,28 +487,28 @@
     wide = sd(q.shape, BF16)
     scratch = pltpu.VMEM
     sems = [
-        (6,), (1,), (nz - 1,), (2, nz // 2), (nx - 1,), (4,), (2, nz - 1), (2, nx - 1), (2,),
-        (2, nx - 1), (2, 2, nz // 2),
+        (6,), (1,), (nz - 1,), (2, 2, nz // 2), (nx - 1,), (4,), (2, nz - 1), (2, nx - 1), (2,),
+        (2, nx - 1), (nz - 1,), (2, 2, nz // 2),
     ]
     outs = pl.pallas_call(
         lambda *refs: layer_kernel(nx, nz, *refs),
         out_shape=(wide, wide, wide, rows, rows, sd((2, nz, nx, HD, HD), BF16)),
-        in_specs=vmem(7), out_specs=tuple(vmem(6)),
+        in_specs=[pl.BlockSpec(memory_space=pltpu.HBM)] * 7, out_specs=tuple(vmem(6)),
         scratch_shapes=[
-            scratch((4, T, HD), BF16), scratch((2, 2, T), F32),
+            scratch((2, 4, T, HD), BF16), scratch((2, 2, 2, T), F32),
             scratch((nz, T, layer_input.shape[1]), BF16),
             scratch((2, T, T), F32), scratch((2, T, 2 * HD), F32), scratch((2, T, HD), F32),
             scratch((2, 3 * HD, HD), F32), scratch((nz, 3 * HD, HD), F32),
             scratch((2, 3 * HD, HD), F32), scratch((2, 3 * HD, HD), F32), scratch((3, 3 * HD, HD), F32),
             scratch((nx, 3 * HD, HD), F32), scratch((nx + 1, HD, HD), F32), scratch((nx + 1, HD, HD), F32),
-            scratch((2, 2 * HD, HD), F32),
-            scratch((3, T, HD), BF16), scratch((8, T), F32), scratch((8, T), F32),
+            scratch((2, 2, HD, HD), F32),
+            scratch((2, 3, T, HD), BF16), scratch((2, 8, T), F32), scratch((8, T), F32),
             scratch((2, nz, T, HD), BF16), scratch((2, nx, HD, HD), BF16), scratch((2, nx, HD, HD), BF16),
-            scratch((2, 2, HD, HD), BF16),
+            scratch((2, 2, HD, HD), BF16), pltpu.SemaphoreType.DMA((6,)),
         ]
         + [pltpu.SemaphoreType.DMA(shape) for shape in sems for _ in range(2)],
         compiler_params=pltpu.CompilerParams(
-            collective_id=0, has_side_effects=True, vmem_limit_bytes=48 * 2**20
+            collective_id=0, has_side_effects=True, vmem_limit_bytes=62 * 2**20
         ),
         name="layer",
     )(layer_input, q, k, v, do, beta.T, lg.T)

time: 129 us -> 112 us (0.87)
  the two profiles are of different devices: /device:TPU:24 before, /device:TPU:32 now
where the time goes in v3:
time: 112 us
  Pallas kernels  111 us (99%)
    pallas_call x1, Pallas kernels, shards(): pl.pallas_call(lambda *refs: layer_kernel(nx, nz, *refs), out_shape=(wide...  108 us
    pallas_call x1, Pallas kernels, shards(): pl.pallas_call(finish_kernel, out_shape=(wide, wide, wide, rows, rows, sd...  3.44 us

profile of v3, /device:TPU:32, one launch (start us, length us, event | category | flops | bytes accessed | tf_op | source)
XLA Modules:
  0.0 111.9 jit_solution(14105308681669504371)
XLA Ops:
  0.6 107.8 %layer.1 = (bf16[128,256]{1,0:T(8,128)(2,1)}, bf16[128,256]{1,0:T(8,128)(2,1)}, bf16[128,256]{1,0:T(8,128)(2,1)}, f32[2,128]{1,0:T(2,128)}, f32[2,128]{1,0:T(2,128)}, /*index=5*/bf16[2,8,4,128,128]{4,3,2,1,0:T(8,128)(2,1)}) custom-call(bf16[128,512]{1,0:T(8,128)(2,1)} %refs_0_.1, bf16[128,256]{1,0:T(8,128)(2,1)} %refs_1_.1, bf16[128,256]{1,0:T(8,128)(2,1)} %refs_2_.1, ...), custom_call_target="tpu_custom_call" | custom-call | tf_op jit(solution)/shard_map/layer/pallas_call | solution.py:493
  108.4 3.4 %finish.1 = (bf16[128,256]{1,0:T(8,128)(2,1)}, bf16[128,256]{1,0:T(8,128)(2,1)}, bf16[128,256]{1,0:T(8,128)(2,1)}, f32[2,128]{1,0:T(2,128)}, f32[2,128]{1,0:T(2,128)}, /*index=5*/bf16[4096,256]{1,0:T(8,128)(2,1)}) custom-call(bf16[128,256]{1,0:T(8,128)(2,1)} %get-tuple-element.18.refs_0_, bf16[128,256]{1,0:T(8,128)(2,1)} %get-tuple-element.19.refs_1_, ...), custom_call_target="tpu_custom_call" | custom-call | tf_op jit(solution)/shard_map/finish/pallas_call | solution.py:515

commit v4 on v3

--- a/solution.py
+++ b/solution.py
@@ -85,14 +85,18 @@
     return (a, b, c), (inverse, uw, back)
 
 
-def local_grads(q, k, v, do, beta_row, lg_row, inverse, uw, back, state, adj):
+def local_update(k, beta_row, lg_row, inverse, uw, back, state, adj):
+    tail = gate_parts(lg_row)[2]
+    update = uw[:, :HD] - dot(uw[:, HD:], state)
+    e = dot(inverse, back + dot(tail * k.astype(F32), adj), 0, 0)
+    return update, e, as_column(beta_row) * e
+
+
+def local_grads(q, k, v, do, beta_row, lg_row, update, e, state, adj):
     line, col = iotas()
     beta = as_column(beta_row)
     decay, growth, tail, keep = gate_parts(lg_row)
     queries, keys, values, grads = (m.astype(F32) for m in (q, k, v, do))
-    update = uw[:, :HD] - dot(uw[:, HD:], state)
-    d_update = back + dot(tail * keys, adj)
-    e = dot(inverse, d_update, 0, 0)
     de = jnp.concatenate([grads, e], 0)
     by_state = dot(de, state, 1, 1)
     by_update = dot(de, update, 1, 1)
@@ -108,14 +112,13 @@
     tail_nz = tail * nz
     dk_col = crossed + tail_nz
     dk_row = beta * r
-    dv = beta * e
     d_beta = jnp.sum(e * values + keys * r, axis=1, keepdims=True)
     d_run = jnp.sum(queries * dq + keys * (dk_row - dk_col), axis=1, keepdims=True)
     last = jnp.sum(tail_nz * keys, axis=(0, 1), keepdims=True) + keep * jnp.sum(
         adj * state, axis=(0, 1), keepdims=True
     )
     d_lg = jnp.sum(jnp.where(line >= col, d_run, 0.0), axis=0, keepdims=True) + last
-    return dq, dk_row + dk_col, dv, as_row(d_beta), d_lg
+    return dq, dk_row + dk_col, as_row(d_beta), d_lg
 
 
 class Place:
@@ -229,11 +232,11 @@
 def layer_kernel(
     nx, nz, li, q, k, v, do, beta, lg, dq, dk, dv, d_beta, d_lg, dw,
     inp, gates, xg, inverse, uw, back, pair, zbuf, left, right, joined, xbuf, xf, xb, both,
-    ret, ret_gate, got_gate, g, psend, precv, ybuf, load_sems, *sem_refs
+    written, ret, ret_gate, got_gate, g, psend, precv, ybuf, load_sems, *sem_refs
 ):
-    in_s, sw_s, hd_s, z_s, x_s, ret_s, g_s, p_s, y_s, ax_s, an_s, az_s = (
+    in_s, sw_s, hd_s, z_s, x_s, ret_s, g_s, p_s, y_s, ax_s, an_s, az_s, aw_s = (
         (lambda a, b: lambda *i: (a.at[i], b.at[i]))(sem_refs[2 * n], sem_refs[2 * n + 1])
-        for n in range(12)
+        for n in range(13)
     )
     place = Place(nx, nz)
     x, z, y, h = place.x, place.z, place.y, place.h
@@ -350,28 +353,41 @@
         remote(ret_gate.at[1], got_gate, ret_s(3), place.partner()),
     ]
 
+    def update_of(turn, carry):
+        n = 1 - turn
+        slot = lax.rem(y + n, 2)
+        parts = inputs(n)
+        update, e, gv = local_update(
+            parts[1], parts[4], parts[5], inverse[n], uw[n], back[n], both[slot, 0], both[slot, 1]
+        )
+        written[n, 0] = update
+        written[n, 1] = e
+        ret[n, 2] = gv.astype(BF16)
+
+        @pl.when(turn == 0)
+        def _():
+            for copy in given:
+                copy.start()
+
+        return carry
+
     def grads_of(turn, carry):
         n = 1 - turn
         slot = lax.rem(y + n, 2)
-        gq, gk, gv, gb, gl = local_grads(
-            *inputs(n), inverse[n], uw[n], back[n], both[slot, 0], both[slot, 1]
+        gq, gk, gb, gl = local_grads(
+            *inputs(n), written[n, 0], written[n, 1], both[slot, 0], both[slot, 1]
         )
         ret[n, 0] = gq.astype(BF16)
         ret[n, 1] = gk.astype(BF16)
-        ret[n, 2] = gv.astype(BF16)
         ret_gate[n, 0:1] = gb
         ret_gate[n, 1:2] = gl
 
         @pl.when(turn == 0)
         def _():
-            for copy in given + returned:
+            for copy in returned:
                 copy.start()
 
         return carry
-
-    lax.fori_loop(0, 2, grads_of, 0)
-    sent += given + returned
-    g[0, z] = ret[0, 2]
 
     def share(p):
         return begin(
@@ -382,7 +398,11 @@
             sent,
         )
 
+    lax.fori_loop(0, 2, update_of, 0)
+    g[0, z] = ret[0, 2]
     shared = [share(0)]
+    lax.fori_loop(0, 2, grads_of, 0)
+    sent += given + returned
     arrive(given)
     shared.append(share(1))
     dq[:, mine] = ret[0, 0]
@@ -436,7 +456,7 @@
     one, two = y, 1 - y
     piece = dw.at[one, chunk(z), x]
     by_x = begin(
-        [remote(piece, piece, ax_s(0, t - 1), place.at(x=place.other_x(t))) for t in range(1, nx)],
+        [remote(piece, piece, ax_s(t - 1), place.at(x=place.other_x(t))) for t in range(1, nx)],
         sent,
     )
     piece = dw.at[two, chunk(z), x]
@@ -447,20 +467,36 @@
     wide = ring_z(
         place, lambda slot, part: dw.at[one, chunk(slot), pl.ds(part * half, half)], az_s, sent
     )
+    passed = []
+
+    def pass_on(t):
+        piece = dw.at[two, chunk(lax.rem(z + nz - t, nz)), x]
+        passed.extend(
+            begin(
+                [
+                    remote(piece, piece, aw_s(t, n - 1), place.at(x=place.other_x(n)))
+                    for n in range(1, nx)
+                ],
+                sent,
+            )
+        )
+
+    near = [t for n in range(1, nz // 2) for t in (n, nz - n)] + [nz // 2]
+    pass_on(0)
+    for t in near[:2]:
+        by_z[t - 1].wait_recv()
+        pass_on(t)
     arrive(by_x)
     next(wide)
-    arrive(by_z)
-    pieces = dw.at[two, :, x]
-    by_x = begin(
-        [remote(pieces, pieces, ax_s(1, t - 1), place.at(x=place.other_x(t))) for t in range(1, nx)],
-        sent,
-    )
+    for t in near[2:]:
+        by_z[t - 1].wait_recv()
+        pass_on(t)
     for _ in wide:
         pass
     arrive(returned)
     d_beta[pl.ds(1 - y, 1), :] = got_gate[0:1]
     d_lg[pl.ds(1 - y, 1), :] = got_gate[1:2]
-    arrive(by_x)
+    arrive(passed)
     for copy in sent:
         copy.wait_send()
 
@@ -488,7 +524,7 @@
     scratch = pltpu.VMEM
     sems = [
         (6,), (1,), (nz - 1,), (2, 2, nz // 2), (nx - 1,), (4,), (2, nz - 1), (2, nx - 1), (2,),
-        (2, nx - 1), (nz - 1,), (2, 2, nz // 2),
+        (nx - 1,), (nz - 1,), (2, 2, nz // 2), (nz, nx - 1),
     ]
     outs = pl.pallas_call(
         lambda *refs: layer_kernel(nx, nz, *refs),
@@ -502,20 +538,21 @@
             scratch((2, 3 * HD, HD), F32), scratch((2, 3 * HD, HD), F32), scratch((3, 3 * HD, HD), F32),
             scratch((nx, 3 * HD, HD), F32), scratch((nx + 1, HD, HD), F32), scratch((nx + 1, HD, HD), F32),
             scratch((2, 2, HD, HD), F32),
-            scratch((2, 3, T, HD), BF16), scratch((2, 8, T), F32), scratch((8, T), F32),
+            scratch((2, 2, T, HD), F32), scratch((2, 3, T, HD), BF16), scratch((2, 8, T), F32), scratch((8, T), F32),
             scratch((2, nz, T, HD), BF16), scratch((2, nx, HD, HD), BF16), scratch((2, nx, HD, HD), BF16),
             scratch((2, 2, HD, HD), BF16), pltpu.SemaphoreType.DMA((6,)),
         ]
         + [pltpu.SemaphoreType.DMA(shape) for shape in sems for _ in range(2)],
         compiler_params=pltpu.CompilerParams(
-            collective_id=0, has_side_effects=True, vmem_limit_bytes=62 * 2**20
+            collective_id=0, has_side_effects=True, vmem_limit_bytes=48 * 2**20
         ),
         name="layer",
-    )(layer_input, q, k, v, do, beta.T, lg.T)
+    )(*(pltpu.with_memory_space_constraint(a, pltpu.HBM) for a in (layer_input, q, k, v, do, beta.T, lg.T)))
     dq, dk, dv, d_beta, d_lg, dw = pl.pallas_call(
         finish_kernel,
         out_shape=(wide, wide, wide, rows, rows, sd((nz * nx * HD, v.shape[1]), BF16)),
-        in_specs=vmem(6), out_specs=tuple(vmem(6)), name="finish",
+        in_specs=vmem(6), out_specs=tuple(vmem(6)),
+        compiler_params=pltpu.CompilerParams(vmem_limit_bytes=12 * 2**20), name="finish",
     )(*outs)
     return dq, dk, dv, d_beta.T, d_lg.T, dw
 

time: 112 us -> 109 us (0.973)
  the two profiles are of different devices: /device:TPU:32 before, /device:TPU:16 now
where the time goes in v4:
time: 109 us
  Pallas kernels  108 us (99%)
    pallas_call x1, Pallas kernels, shards(): pl.pallas_call(lambda *refs: layer_kernel(nx, nz, *refs), out_shape=(wide...  106 us

profile of v4, /device:TPU:16, one launch (start us, length us, event | category | flops | bytes accessed | tf_op | source)
XLA Modules:
  0.0 108.8 jit_solution(1431469766294186141)
XLA Ops:
  0.6 106.4 %layer.1 = (bf16[128,256]{1,0:T(8,128)(2,1)S(1)}, bf16[128,256]{1,0:T(8,128)(2,1)S(1)}, bf16[128,256]{1,0:T(8,128)(2,1)S(1)}, f32[2,128]{1,0:T(2,128)S(1)}, f32[...) custom-call(bf16[128,512]{1,0:T(8,128)(2,1)} %refs_0_.1, bf16[128,256]{1,0:T(8,128)(2,1)} %refs_1_.1, ...), custom_call_target="tpu_custom_call" | custom-call | tf_op jit(solution)/shard_map/layer/pallas_call | solution.py:529
  107.1 1.8 %finish.1 = (bf16[128,256]{1,0:T(8,128)(2,1)}, bf16[128,256]{1,0:T(8,128)(2,1)}, bf16[128,256]{1,0:T(8,128)(2,1)}, f32[2,128]{1,0:T(2,128)}, f32[2,128]{1,0:T(2,128)}, /*index=5*/bf16[4096,256]{1,0:T(8,128)(2,1)}) custom-call(bf16[128,256]{1,0:T(8,128)(2,1)S(1)} %get-tuple-element.18.refs_0_, bf16[128,256]{1,0:T(8,128)(2,1)S(1)} %get-tuple-element.19.refs_1_, ...), custom_call_target="tpu_custom_call" | custom-call | tf_op jit(solution)/shard_map/finish/pallas_call | solution.py:551

commit v5 on v4

--- a/solution.py
+++ b/solution.py
@@ -314,17 +314,12 @@
             compose(acc, zbuf.at[lax.rem(z + t, nz)], acc)
 
     for t in ring_z(place, zview, z_s, sent):
-        if t == 1:
-            arrive(swapped)
-            spread = begin(
-                [
-                    remote(xg.at[h], xg.at[h], hd_s(n - 1), place.along_head(n))
-                    for n in range(1, nz)
-                ],
-                sent,
-            )
-        else:
+        if t > 1:
             fold(t - 1)
+    arrive(swapped)
+    spread = begin(
+        [remote(xg.at[h], xg.at[h], hd_s(n - 1), place.along_head(n)) for n in range(1, nz)], sent
+    )
     fold(nz // 2)
     compose(joined.at[0], left.at[0], right.at[1])
     compose(joined.at[1], left.at[1], right.at[0])

time: 109 us -> 112 us (1.028)
  the two profiles are of different devices: /device:TPU:16 before, /device:TPU:24 now
where the time goes in v5:
time: 112 us
  Pallas kernels  111 us (99%)
    pallas_call x1, Pallas kernels, shards(): pl.pallas_call(lambda *refs: layer_kernel(nx, nz, *refs), out_shape=(wide...  109 us

profile of v5, /device:TPU:24, one launch (start us, length us, event | category | flops | bytes accessed | tf_op | source)
XLA Modules:
  0.0 111.7 jit_solution(12748439174817817184)
XLA Ops:
  0.6 109.3 %layer.1 = (bf16[128,256]{1,0:T(8,128)(2,1)S(1)}, bf16[128,256]{1,0:T(8,128)(2,1)S(1)}, bf16[128,256]{1,0:T(8,128)(2,1)S(1)}, f32[2,128]{1,0:T(2,128)S(1)}, f32[...) custom-call(bf16[128,512]{1,0:T(8,128)(2,1)} %refs_0_.1, bf16[128,256]{1,0:T(8,128)(2,1)} %refs_1_.1, ...), custom_call_target="tpu_custom_call" | custom-call | tf_op jit(solution)/shard_map/layer/pallas_call | solution.py:524
  110.0 1.8 %finish.1 = (bf16[128,256]{1,0:T(8,128)(2,1)}, bf16[128,256]{1,0:T(8,128)(2,1)}, bf16[128,256]{1,0:T(8,128)(2,1)}, f32[2,128]{1,0:T(2,128)}, f32[2,128]{1,0:T(2,128)}, /*index=5*/bf16[4096,256]{1,0:T(8,128)(2,1)}) custom-call(bf16[128,256]{1,0:T(8,128)(2,1)S(1)} %get-tuple-element.18.refs_0_, bf16[128,256]{1,0:T(8,128)(2,1)S(1)} %get-tuple-element.19.refs_1_, ...), custom_call_target="tpu_custom_call" | custom-call | tf_op jit(solution)/shard_map/finish/pallas_call | solution.py:546
